TPU v7x, 512 devices: a whole 4x4x16 slice. The times are simulated.
512 devices in a mesh: pairs: 128 (over x, z, core), ints: 4 (over y).
Axes of the slice: x: 4, y: 4, z: 16, core: 2. Of those that a mesh axis runs over, the one named last changes fastest.
Arguments:
- amps: float32 [256, 256, 256], P('pairs', 'ints'), may hold values from -0.8 to 0.8
- resid_rest: float32 [256, 256, 256], P('pairs', 'ints'), may hold values from -6 to 6
- int_blocks: bfloat16 [128, 256, 256], P('pairs'), may hold values from -0.375 to 0.375
- virt_energy: float32 [256, 256], P('pairs'), may hold values from 0.5 to 3
- pair_energy: float32 [256], P('pairs'), may hold values from -2 to -0.5
- item_block: int32 [32768, 1], P(('pairs', 'ints')), may hold values from 0 to 127; in each aligned block of 64 rows (0 to 63, 64 to 127, ...) at most 2 rows name the same one
- share_owner: int32 [12288, 1], P('pairs'), may hold values from 0 to 127; in each aligned block of 96 rows (0 to 95, 96 to 191, ...) at most 2 rows name the same one
- share_pair: int32 [12288, 1], P('pairs'), may hold values from 0 to 1
- share_amp: int32 [12288, 1], P('pairs'), may hold values from 0 to 1
- transpose_pair: int32 [256], P('pairs'), may hold values from 0 to 255, as said below
Outputs:
- update: float32 [256, 256, 256], P('pairs', 'ints')
Inputs may be any that keep to these rules, and one draw needn't show every extreme that they name: `item_block`: within each aligned block of 64 rows no value occurs more than 2 times, and some value occurs exactly 2 times. `share_owner`: within each aligned block of 96 rows no value occurs more than 2 times, and some value occurs exactly 2 times. `transpose_pair`: A permutation equal to its own inverse; pair p maps into the block of 2 consecutive pairs whose block number is (p // 2 + 256 // 4) modulo 256 // 2.
All inputs are finite; a program needn't handle non-finite values.
Results may differ from a plain program's by a relative error of at most 0.008.
Values may be sent and summed in bfloat16 or wider, within the bound.
A program may use at most 64 MiB of HBM per device.

v0:
```python
import jax
import jax.numpy as jnp
from jax import lax
from jax.sharding import Mesh
from jax.sharding import PartitionSpec as P

PAIRS = ("pairs_0", "pairs_1", "pairs_2")
PAIRS_INTS = ("pairs_0", "pairs_1", "pairs_2", "ints")


def in_blocks(array, dim, size):
    before, after = (array.shape[:dim], array.shape[dim + 1 :])
    return jnp.moveaxis(array.reshape(*before, size, -1, *after), dim, 0)


def sum_at_owner(array, axis, dim):
    tiles = in_blocks(array, dim, lax.axis_size(axis))
    arrived = lax.all_to_all(tiles, axis, split_axis=0, concat_axis=0, tiled=True)
    return arrived.astype(jnp.float32).sum(axis=0)


def laid_out(tiles, dim):
    dims = list(tiles.shape[1:])
    dims[dim] *= tiles.shape[0]
    return jnp.moveaxis(tiles, 0, dim).reshape(dims)


def stacked_from(array, axes, order):
    tiles = array
    for k in order:
        tiles = lax.all_gather(tiles, axes[k])
    done = order[::-1]
    back = [done.index(k) for k in range(len(axes))]
    tiles = tiles.transpose(*back, *range(len(axes), tiles.ndim))
    return tiles.reshape(-1, *array.shape)


def gather_axes(array, axes, order, dim):
    return laid_out(stacked_from(array, axes, order), dim)


def from_behind(value, axis, steps):
    count = lax.axis_size(axis)
    pairs = [(source, (source + steps) % count) for source in range(count)]
    return lax.ppermute(value, axis, pairs)


def slot_ranks(targets, n_groups):
    match_hits = (targets[:, None] == jnp.arange(n_groups, dtype=jnp.int32)[None, :]).astype(
        jnp.int32
    )
    before = jnp.cumsum(match_hits, axis=0) - match_hits
    return jnp.sum(before * match_hits, axis=1)


def body(
    amps,
    resid_rest,
    int_blocks,
    virt_energy,
    pair_energy,
    item_block,
    share_owner,
    share_pair,
    share_amp,
    transpose_pair,
):
    n_pairs = lax.axis_size(PAIRS)
    pair_index = lax.axis_index(PAIRS)
    quarter = lax.axis_index("ints")
    pair_count, row_count, domain = amps.shape
    amp_half = amps.astype(jnp.bfloat16)
    n_items = item_block.shape[0]
    item_height = pair_count * row_count // n_items
    item_rows = amp_half.reshape(n_items, item_height, domain)
    block_targets = item_block[:, 0]
    cap_items = max(2, 3 * n_items // (2 * n_pairs))
    item_slot = block_targets * cap_items + slot_ranks(block_targets, n_pairs)
    outgoing = (
        jnp.zeros((n_pairs * cap_items, item_height, domain), jnp.bfloat16)
        .at[item_slot]
        .set(item_rows)
    )
    outgoing = outgoing.reshape(n_pairs, cap_items, item_height, domain)
    resident = int_blocks[0]
    arrived = lax.all_to_all(outgoing, PAIRS, split_axis=0, concat_axis=0, tiled=True)
    leading = arrived.shape[:3]
    product = jnp.dot(arrived.reshape(-1, domain), resident, preferred_element_type=jnp.float32)
    product = product.astype(jnp.bfloat16).reshape(leading + (domain,))
    returned = lax.all_to_all(product, PAIRS, split_axis=0, concat_axis=0, tiled=True)
    x_rows = returned.reshape(n_pairs * cap_items, item_height, domain)[item_slot]
    x_rows = x_rows.reshape(pair_count, row_count, domain)
    partial_value = jnp.einsum("pac,pad->pcd", amp_half, x_rows, preferred_element_type=jnp.float32)
    intermed = sum_at_owner(partial_value.astype(jnp.bfloat16), "ints", 1).astype(jnp.bfloat16)
    amp_full = lax.all_gather(amp_half, "ints", axis=1, tiled=True)
    owners = share_owner[:, 0]
    wanted = share_pair[:, 0]
    n_req = owners.shape[0]
    per_pair = n_req // pair_count
    source_global = owners * pair_count + wanted
    empty_rows = jnp.zeros((n_req, row_count, domain), jnp.bfloat16)
    piece = gather_axes(intermed, PAIRS, (0, 1, 2), 0)
    start = jnp.int32(0)
    local = jnp.clip(source_global, 0, piece.shape[0] - 1)
    inside = (source_global >= start) & (source_global < start + piece.shape[0])
    picked = jnp.where(inside[:, None, None], piece[local], empty_rows)
    picked = picked.reshape(pair_count, per_pair, row_count, domain)
    partners = share_amp[:, 0].reshape(pair_count, per_pair)

    def cycle_one(packed):
        w_req, amp_index = packed
        return jnp.einsum(
            "kac,kcb->ab", w_req, amp_full[amp_index], preferred_element_type=jnp.float32
        )

    cycle_term = lax.map(cycle_one, (picked, partners))
    energies_rows = lax.dynamic_slice_in_dim(virt_energy, quarter * row_count, row_count, 1)
    divisor = energies_rows[:, :, None] + virt_energy[:, None, :] - pair_energy[:, None, None]
    scaled = (resid_rest + cycle_term) / divisor
    mirror_part = from_behind(scaled.astype(jnp.bfloat16), PAIRS, n_pairs // 2).astype(scaled.dtype)
    turned = lax.all_to_all(
        mirror_part.astype(jnp.bfloat16), "ints", split_axis=2, concat_axis=1, tiled=True
    ).astype(mirror_part.dtype)
    partner_dev = (pair_index + n_pairs // 2) % n_pairs
    local_swap = transpose_pair - partner_dev * pair_count
    mirrored = jnp.transpose(turned[local_swap], (0, 2, 1))
    return -0.5 * (scaled + mirrored)


def solution(mesh):
    torus = Mesh(
        mesh.devices.reshape(4, 16, 2, mesh.shape["ints"]),
        ("pairs_0", "pairs_1", "pairs_2", "ints"),
    )
    return jax.shard_map(
        body,
        mesh=torus,
        in_specs=(
            P(PAIRS, "ints", None),
            P(PAIRS, "ints", None),
            P(PAIRS, None, None),
            P(PAIRS, None),
            P(PAIRS),
            P(PAIRS_INTS, None),
            P(PAIRS, None),
            P(PAIRS, None),
            P(PAIRS, None),
            P(PAIRS),
        ),
        out_specs=P(PAIRS, "ints", None),
        check_vma=False,
    )
```

profile of v0, /device:TPU:1, one launch (start us, length us, event | category | flops | bytes accessed | tf_op | source)
XLA Modules:
  0.0 271.9 jit_solution(6148034309779576829)
XLA Ops:
  6.5 0.8 fusion.14
  7.4 0.8 select_reduce_fusion
  8.2 0.7 fusion.15
  8.9 0.9 convert_element_type.35
  10.0 2.4 scatter_fusion
  12.4 42.6 %all_to_all.24 = bf16[128,2,2,256]{3,2,1,0:T(2,128)(2,1)S(1)} all-to-all(bf16[128,2,2,256]{3,2,1,0:T(2,128)(2,1)S(1)} %bitcast.79), channel_id=1, replica_groups=mesh['pairs_0'=4,'pairs_1'=16,'pairs_2'=2,'ints'=4] {'pairs_0','pairs_1'..., dimensions={0} | all-to-all | bytes 524288 | tf_op jit(solution)/shard_map/all_to_all | solution.py:86
  55.4 0.8 reshape.85
  56.2 7.4 %all-to-all-start.1 = ((bf16[128,2,2,256]{3,2,1,0:T(2,128)(2,1)}), bf16[128,2,2,256]{3,2,1,0:T(2,128)(2,1)S(1)}, u32[]{:S(2)}, u32[]{:S(2)}) async-start(bf16[128,2,2,256]{3,2,1,0:T(2,128)(2,1)} %reshape.85), calls=%async_computation.1 | async-start | bytes 524288 | tf_op jit(solution)/shard_map/all_to_all | solution.py:90
  63.6 22.4 %all-to-all-done.1 = bf16[128,2,2,256]{3,2,1,0:T(2,128)(2,1)S(1)} async-done(((bf16[128,2,2,256]{3,2,1,0:T(2,128)(2,1)}), bf16[128,2,2,256]{3,2,1,0:T(2,128)(2,1)S(1)}, u32[]{:S(2)}, u32[]{:S(2)}) %all-to-all-start.1) | async-done | bytes 262176 | tf_op jit(solution)/shard_map/all_to_all | solution.py:90
  86.0 0.7 gather_fusion.1
  87.1 9.5 %all_to_all.25 = bf16[4,2,64,256]{3,2,1,0:T(8,128)(2,1)S(1)} all-to-all(bf16[4,2,64,256]{3,2,1,0:T(8,128)(2,1)S(1)} %bitcast.83), channel_id=1, replica_groups=mesh['pairs_0'=4,'pairs_1'=16,'pairs_2'=2,'ints'=4] {'ints'}, dimensions={0} | all-to-all | bytes 524288 | tf_op jit(solution)/shard_map/all_to_all | solution.py:18
  96.7 10.1 %all-gather = bf16[8,64,256]{2,1,0:T(8,128)(2,1)} all-gather(bf16[2,64,256]{2,1,0:T(8,128)(2,1)S(1)} %reduce_sum.25), channel_id=2, replica_groups=mesh['pairs_0'=4,'pairs_1'=16,'pairs_2'=2,'ints'=4] {'pairs_0'}, dimensions={0}, use_global_device_ids=true | all-gather | bytes 327680 | tf_op jit(solution)/shard_map/all_gather | solution.py:31
  106.9 63.5 %all-gather.6.cloned.1.call-done = bf16[64,2,64,256]{3,2,1,0:T(8,128)(2,1)} async-done(((bf16[4,2,64,256]{3,2,1,0:T(8,128)(2,1)}), bf16[64,2,64,256]{3,2,1,0:T(8,128)(2,1)}) %all-gather.6.cloned.1.call-update) | async-done | bytes 4194320 | tf_op jit(solution)/shard_map/all_gather | solution.py:31
  172.5 10.1 %all_gather.27 = bf16[2,256,256]{2,1,0:T(8,128)(2,1)S(1)} all-gather(bf16[2,64,256]{2,1,0:T(8,128)(2,1)S(1)} %convert_element_type.35), channel_id=1, replica_groups=mesh['pairs_0'=4,'pairs_1'=16,'pairs_2'=2,'ints'=4] {'ints'}, dimensions={1}, use_global_device_ids=true | all-gather | bytes 327680 | tf_op jit(solution)/shard_map/all_gather | solution.py:95
  182.7 26.8 %all-gather.8.cloned.1.call-done = bf16[32,4,2,64,256]{4,3,2,1,0:T(8,128)(2,1)} async-done(((bf16[16,4,2,64,256]{4,3,2,1,0:T(8,128)(2,1)}), bf16[32,4,2,64,256]{4,3,2,1,0:T(8,128)(2,1)}) %all-gather.8.cloned.1.call-update) | async-done | bytes 8388624 | tf_op jit(solution)/shard_map/all_gather | solution.py:31
  209.5 8.3 %copy.15 = bf16[4,16,2,2,64,256]{5,4,3,2,1,0:T(8,128)(2,1)} copy(bf16[4,16,2,2,64,256]{5,4,3,0,1,2:T(8,128)(2,1)} %bitcast.77) | data formatting | bytes 16777216 | tf_op jit(solution)/shard_map/transpose | solution.py:34
  217.7 5.9 %gather_fusion.2 = bf16[96,64,256]{2,1,0:T(8,128)(2,1)} fusion(bf16[256,64,256]{2,1,0:T(8,128)(2,1)} %bitcast.75, s32[1024]{0:T(1024)S(1)} %pad_clamp_fusion.2), kind=kCustom, calls=%fused_computation.2 | custom fusion | bytes 6291840 | tf_op jit(solution)/shard_map/gather | solution.py:106
  223.7 2.2 broadcast_select_fusion
  225.9 20.2 %while.10 = (s32[]{:T(128)}, f32[2,64,256]{2,1,0:T(8,128)}, bf16[2,48,64,256]{3,2,1,0:T(8,128)(2,1)S(1)}, s32[2,48]{1,0:T(2,128)}, bf16[2,256,256]{2,1,0:T(8,128)(2,1)S(1)}, /*index=5*/s32[]{:T(128)}) while((s32[]{:T(128)}, f32[2,64,256]{2,1,0:T(8,128)}, bf16[2,48,64,256]{3,2,1,0:T(8,128)(2,1)S(1)}, s32[2,48]{1,0:T(2,128)}, ...), condition=%wide.region_5.6_spmd, body=%wide.region_4.5_spmd.sunk | while | flops 402654368 | bytes 20518728 | solution.py:116
  225.9 0.6 fusion.28
  226.5 4.8 %gather_fusion = bf16[48,256,256]{2,1,0:T(8,128)(2,1)} fusion(bf16[2,256,256]{2,1,0:T(8,128)(2,1)S(1)} %get-tuple-element.90, s32[1024]{0:T(1024)S(1)} %pad_clamp_fusion.5), kind=kCustom, calls=%fused_computation.clone.1 | custom fusion | bytes 12583104 | tf_op jit(solution)/shard_map/while/body/eval_jaxpr/gather | solution.py:113
  231.3 4.6 %fusion.29 = f32[2,64,256]{2,1,0:T(8,128)} fusion(f32[2,64,256]{2,1,0:T(8,128)} %get-tuple-element.81, s32[]{:T(128)} %get-tuple-element.80, bf16[48,256,256]{2,1,0:T(8,128)(2,1)} %gather_fusion, bf16[2,48,64,256]{3,2,1,0:T(8,128)(2,1)S(1)} %get-tuple-element.88), kind=kOutput, calls=%fused_computation.9.clone.1 | convolution fusion | flops 402653184 | bytes 7930880 | tf_op jit(solution)/shard_map/while/body/eval_jaxpr/kac,kcb->ab/dot_general | solution.py:112
  236.6 4.8 %gather_fusion = bf16[48,256,256]{2,1,0:T(8,128)(2,1)} fusion(bf16[2,256,256]{2,1,0:T(8,128)(2,1)S(1)} %get-tuple-element.90, s32[1024]{0:T(1024)S(1)} %pad_clamp_fusion.5), kind=kCustom, calls=%fused_computation.clone.1 | custom fusion | bytes 12583104 | tf_op jit(solution)/shard_map/while/body/eval_jaxpr/gather | solution.py:113
  241.4 4.6 %fusion.29 = f32[2,64,256]{2,1,0:T(8,128)} fusion(f32[2,64,256]{2,1,0:T(8,128)} %get-tuple-element.81, s32[]{:T(128)} %get-tuple-element.80, bf16[48,256,256]{2,1,0:T(8,128)(2,1)} %gather_fusion, bf16[2,48,64,256]{3,2,1,0:T(8,128)(2,1)S(1)} %get-tuple-element.88), kind=kOutput, calls=%fused_computation.9.clone.1 | convolution fusion | flops 402653184 | bytes 7930880 | tf_op jit(solution)/shard_map/while/body/eval_jaxpr/kac,kcb->ab/dot_general | solution.py:112
  246.0 1.1 fusion.17
  247.1 3.7 %collective-permute-start = (bf16[2,64,256]{2,1,0:T(8,128)(2,1)S(1)}, bf16[2,64,256]{2,1,0:T(8,128)(2,1)S(1)}, u32[]{:S(2)}, u32[]{:S(2)}) collective-permute-start(bf16[2,64,256]{2,1,0:T(8,128)(2,1)S(1)} %fusion.17), channel_id=1, source_target_pairs={{0,256},{4,260},{8,264},{12,268},{16,272},{20,276},{24,280},{28,28... | collective-permute-start | bytes 196616 | tf_op jit(solution)/shard_map/ppermute | solution.py:45
  250.8 0.7 compare_select_fusion.1
  251.4 2.2 collective-permute-done
  253.7 0.8 reshape.152
  254.5 3.3 %all-to-all-start.3 = ((bf16[4,2,4096]{2,1,0:T(2,128)(2,1)}), bf16[4,2,4096]{2,1,0:T(2,128)(2,1)S(1)}, u32[]{:S(2)}, u32[]{:S(2)}) async-start(bf16[4,2,4096]{2,1,0:T(2,128)(2,1)} %reshape.152), calls=%async_computation.3 | async-start | bytes 131072 | tf_op jit(solution)/shard_map/all_to_all | solution.py:121
  257.8 4.4 %all-to-all-done.3 = bf16[4,2,4096]{2,1,0:T(2,128)(2,1)S(1)} async-done(((bf16[4,2,4096]{2,1,0:T(2,128)(2,1)}), bf16[4,2,4096]{2,1,0:T(2,128)(2,1)S(1)}, u32[]{:S(2)}, u32[]{:S(2)}) %all-to-all-start.3) | async-done | bytes 65568 | tf_op jit(solution)/shard_map/all_to_all | solution.py:121
  263.3 1.7 fusion.12
  (44 shorter events, 4.9 us)
Async XLA Ops:
  6.5 48.6 %copy-start = (bf16[1,256,256]{2,1,0:T(8,128)(2,1)S(1)}, bf16[1,256,256]{2,1,0:T(8,128)(2,1)}, u32[]{:S(2)}) copy-start(bf16[1,256,256]{2,1,0:T(8,128)(2,1)} %param.14) | copy-start | bytes 393220
  56.2 29.9 %all-to-all-start.1 = ((bf16[128,2,2,256]{3,2,1,0:T(2,128)(2,1)}), bf16[128,2,2,256]{3,2,1,0:T(2,128)(2,1)S(1)}, u32[]{:S(2)}, u32[]{:S(2)}) async-start(bf16[128,2,2,256]{3,2,1,0:T(2,128)(2,1)} %reshape.85), calls=%async_computation.1 | async-start | bytes 524288 | tf_op jit(solution)/shard_map/all_to_all | solution.py:90
  63.5 106.9 %all-gather.6.cloned.1.call-start = ((), (), s32[]{:S(2)}) async-start(), calls=%async_computation.4 | async-start | bytes 4456448 | tf_op jit(solution)/shard_map/all_gather | solution.py:31
  87.1 83.4 %copy-start.4 = (s32[96,1]{0,1:T(1,128)S(1)}, s32[96,1]{0,1:T(1,128)}, u32[]{:S(2)}) copy-start(s32[96,1]{0,1:T(1,128)} %param.19) | copy-start | bytes 1156
  87.1 83.4 %copy-start.5 = (s32[96,1]{0,1:T(1,128)S(1)}, s32[96,1]{0,1:T(1,128)}, u32[]{:S(2)}) copy-start(s32[96,1]{0,1:T(1,128)} %param.18) | copy-start | bytes 1156
  87.1 84.1 %copy-start.3 = (s32[96,1]{0,1:T(1,128)S(1)}, s32[96,1]{0,1:T(1,128)}, u32[]{:S(2)}) copy-start(s32[96,1]{0,1:T(1,128)} %param.20) | copy-start | bytes 1156
  87.1 95.5 %copy-start.1 = (f32[2,256]{1,0:T(2,128)S(1)}, f32[2,256]{1,0:T(2,128)}, u32[]{:S(2)}) copy-start(f32[2,256]{1,0:T(2,128)} %param.15) | copy-start | bytes 6148
  106.8 102.7 %all-gather.8.cloned.1.call-start = ((), (), s32[]{:S(2)}) async-start(), calls=%async_computation.5 | async-start | bytes 12582912 | tf_op jit(solution)/shard_map/all_gather | solution.py:31
  225.8 20.2 %copy-start.2 = (f32[2]{0:T(128)S(1)}, f32[2]{0:T(128)}, u32[]{:S(2)}) copy-start(f32[2]{0:T(128)} %param.16) | copy-start | bytes 28
  247.1 6.5 %collective-permute-start = (bf16[2,64,256]{2,1,0:T(8,128)(2,1)S(1)}, bf16[2,64,256]{2,1,0:T(8,128)(2,1)S(1)}, u32[]{:S(2)}, u32[]{:S(2)}) collective-permute-start(bf16[2,64,256]{2,1,0:T(8,128)(2,1)S(1)} %fusion.17), channel_id=1, source_target_pairs={{0,256},{4,260},{8,264},{12,268},{16,272},{20,276},{24,280},{28,28... | collective-permute-start | bytes 196616 | tf_op jit(solution)/shard_map/ppermute | solution.py:45
  254.5 7.7 %all-to-all-start.3 = ((bf16[4,2,4096]{2,1,0:T(2,128)(2,1)}), bf16[4,2,4096]{2,1,0:T(2,128)(2,1)S(1)}, u32[]{:S(2)}, u32[]{:S(2)}) async-start(bf16[4,2,4096]{2,1,0:T(2,128)(2,1)} %reshape.152), calls=%async_computation.3 | async-start | bytes 131072 | tf_op jit(solution)/shard_map/all_to_all | solution.py:121
Sparse Core Ops, SparseCore 0:
  106.9 63.4 all-gather.5
  172.5 36.9 all-gather.7
where the time goes:
time: 274 us; the launch traced here: 272 us
  waiting for transfers between devices  119 us (43%)
  blocking collectives  72.3 us (26%)
  local copies, waits for them, and re-layouts  31.4 us (11%)
  starting transfers between devices  14.4 us (5%)
  between operations  13.7 us (5%)
  other arithmetic  11 us (4%)
  matrix products  9.72 us (4%)
    all_gather x2, waiting for transfers between devices, stacked_from(): tiles = lax.all_gather(tiles, axes[k])  90.3 us
    all_to_all x1, blocking collectives, body(): lax.all_to_all(outgoing, PAIRS, split_axis=0, concat_axis=0, tiled=True)  42.6 us
    all_to_all x1, waiting for transfers between devices, body(): lax.all_to_all(product, PAIRS, split_axis=0, concat_axis=0, tiled=True)  22.4 us
    all_gather x1, blocking collectives, body(): amp_full = lax.all_gather(amp_half, 'ints', axis=1, tiled=True)  10.1 us
    all_gather x1, blocking collectives, stacked_from(): tiles = lax.all_gather(tiles, axes[k])  10.1 us
    gather x2, local copies, waits for them, and re-layouts, cycle_one(): amp_full[amp_index]  9.6 us
    all_to_all x1, blocking collectives, sum_at_owner(): lax.all_to_all(tiles, axis, split_axis=0, concat_axis=0, tiled=True)  9.52 us
    dot_general x2, matrix products, cycle_one(): jnp.einsum('kac,kcb->ab', w_req, amp_full[amp_index], preferred_element_t...  9.22 us
  transfers between devices with their start and end apart: 5, of which 5 were waited for; matrix products, arithmetic and copies ran while one was open for 1% of the time, Pallas kernels for 0%

commit v1 on v0

v1 whole, which is shorter than its diff:
```python
import functools

import jax
import jax.numpy as jnp
from jax import lax
from jax.experimental import pallas as pl
from jax.experimental.pallas import tpu as pltpu
from jax.sharding import Mesh
from jax.sharding import PartitionSpec as P

PAIRS = ("pairs_0", "pairs_1", "pairs_2")
PAIRS_INTS = ("pairs_0", "pairs_1", "pairs_2", "ints")
MESH = pl.DeviceIdType.MESH
F32 = jnp.float32
BF16 = jnp.bfloat16
NX, NZ, NC, NY = 4, 16, 2, 4
V = 256
SL = V // NY
ROWS = 2 * SL
HALF = SL // 2
CAP = 4
BLK8 = NX * NC
SLOTS = NY * BLK8 * CAP
UNITS = NZ * NC * 2
EB = 16


def iota(shape, dim):
    return lax.broadcasted_iota(jnp.int32, shape, dim)


def dot_nt(a, b):
    return lax.dot_general(a, b, (((1,), (1,)), ((), ())), preferred_element_type=F32)


def dot(a, b):
    return jnp.dot(a, b, preferred_element_type=F32)


def kernel(
    amps_ref,
    resid_ref,
    block_ref,
    ecol_ref,
    erow_ref,
    bcol_ref,
    brow_ref,
    unit_ref,
    mate_ref,
    swap_ref,
    out_ref,
    turned,
    blocks,
    amp_all,
    slot_all,
    counts,
    spread,
    slotted,
    inter_acc,
    inter,
    w_send,
    w_recv,
    scaled,
    m_send,
    m_recv,
    send_sem,
    y_recv,
    s_recv,
    n_recv,
    z_recv,
    xw_recv,
    xh_recv,
    core_recv,
    g_recv,
    gc_recv,
    w_rsem,
    m_rsem,
):
    x = lax.axis_index("pairs_0")
    z = lax.axis_index("pairs_1")
    c = lax.axis_index("pairs_2")
    y = lax.axis_index("ints")
    mate = {"pairs_2": 1 - c}
    x_up = {"pairs_0": lax.rem(x + 1, NX)}
    x_down = {"pairs_0": lax.rem(x + NX - 1, NX)}
    z_up = {"pairs_1": lax.rem(z + 1, NZ)}
    z_down = {"pairs_1": lax.rem(z + NZ - 1, NZ)}

    def at_xy(dx, dy):
        return {"pairs_0": lax.rem(x + dx, NX), "ints": lax.rem(y + dy, NY)}

    def remote(src, dst, ssem, rsem, device):
        return pltpu.make_async_remote_copy(
            src_ref=src, dst_ref=dst, send_sem=ssem, recv_sem=rsem, device_id=device, device_id_type=MESH
        )

    def await_bytes(ref, sem):
        pltpu.make_async_copy(ref, ref, sem).wait()

    barrier = pltpu.get_barrier_semaphore()
    offsets = [(dx, dy) for dx in range(NX) for dy in range(NY) if dx or dy]
    greeted = [z_up, z_down, mate] + [at_xy(dx, dy) for dx, dy in offsets]
    for device in greeted:
        pl.semaphore_signal(barrier, inc=1, device_id=device, device_id_type=MESH)

    turned[...] = jnp.transpose(block_ref[...].astype(F32))
    blocks[x, z, c] = turned[pl.ds(pl.multiple_of(y * SL, SL), SL), :].astype(BF16)
    amp_all[y] = amps_ref[...].astype(BF16)

    col = bcol_ref[...]
    row = brow_ref[...]
    earlier = (col == row) & (iota((ROWS, ROWS), 0) < iota((ROWS, ROWS), 1))
    rank = jnp.sum(earlier.astype(F32), axis=0, keepdims=True)
    z_of = (row >> 1) & (NZ - 1)
    place = z_of * (BLK8 * CAP) + ((row >> 5) * NC + (row & 1)) * CAP
    slot_all[y] = jnp.broadcast_to(place.astype(F32) + rank, (8, ROWS))

    n_req = unit_ref.shape[0]
    hot = (unit_ref[...] == iota((n_req, V), 1)).astype(F32).astype(BF16)
    out_id = iota((16, n_req), 0)
    mine = (iota((16, n_req), 1) // (n_req // 2)) * 2 + mate_ref[...]
    pick = (out_id == mine).astype(F32).astype(BF16)
    counts[x] = dot(pick, hot).astype(BF16)

    pl.semaphore_wait(barrier, len(greeted))

    def send_piece(ref, ssem, rsem, device):
        remote(ref, ref, ssem, rsem, device).start()

    def z_piece(zz, up, down):
        piece = blocks.at[x, zz, c]
        if up is not None:

            @pl.when(up)
            def _():
                send_piece(piece, send_sem.at[0], z_recv.at[zz], z_up)

        if down is not None:

            @pl.when(down)
            def _():
                send_piece(piece, send_sem.at[0], z_recv.at[zz], z_down)

        send_piece(piece, send_sem.at[1], xw_recv.at[0, zz], x_up)
        send_piece(piece, send_sem.at[1], xw_recv.at[1, zz], x_down)
        send_piece(piece, send_sem.at[2], core_recv.at[0], mate)

    z_piece(z, True, True)
    for dy in range(1, NY):
        send_piece(slot_all.at[y], send_sem.at[3], s_recv.at[dy], at_xy(0, dy))
        send_piece(amp_all.at[y], send_sem.at[4], y_recv.at[dy], at_xy(0, dy))
    for dx in range(1, NX):
        send_piece(counts.at[x], send_sem.at[5], n_recv.at[dx], at_xy(dx, 0))

    xl, xr, xo = lax.rem(x + NX - 1, NX), lax.rem(x + 1, NX), lax.rem(x + 2, NX)

    def x_piece(zz):
        await_bytes(blocks.at[xl, zz, c], xw_recv.at[0, zz])
        low = blocks.at[xl, zz, c, pl.ds(0, HALF), :]
        send_piece(low, send_sem.at[1], xh_recv.at[0, zz], x_up)
        send_piece(blocks.at[xl, zz, c], send_sem.at[2], core_recv.at[0], mate)
        await_bytes(blocks.at[xr, zz, c], xw_recv.at[1, zz])
        high = blocks.at[xr, zz, c, pl.ds(HALF, HALF), :]
        send_piece(high, send_sem.at[1], xh_recv.at[1, zz], x_down)
        send_piece(blocks.at[xr, zz, c], send_sem.at[2], core_recv.at[0], mate)

    def far_piece(zz):
        await_bytes(blocks.at[xo, zz, c, pl.ds(0, HALF), :], xh_recv.at[0, zz])
        await_bytes(blocks.at[xo, zz, c, pl.ds(HALF, HALF), :], xh_recv.at[1, zz])
        send_piece(blocks.at[xo, zz, c], send_sem.at[2], core_recv.at[0], mate)

    last = NZ // 2

    def both(s, work):
        @pl.when((s >= 0) & (s <= last))
        def _():
            work(lax.rem(z - s + NZ, NZ))

        @pl.when((s >= 1) & (s < last))
        def _():
            work(lax.rem(z + s, NZ))

    def gather_step(s, carry):
        @pl.when(s <= last)
        def _():
            zz = lax.rem(z - s + NZ, NZ)
            await_bytes(blocks.at[x, zz, c], z_recv.at[zz])
            z_piece(zz, s < last, None)

        @pl.when(s < last)
        def _():
            zz = lax.rem(z + s, NZ)
            await_bytes(blocks.at[x, zz, c], z_recv.at[zz])
            z_piece(zz, None, s < last - 1)

        both(s - 1, x_piece)
        both(s - 2, far_piece)
        return carry

    lax.fori_loop(1, last + 3, gather_step, 0)

    for dy in range(1, NY):
        other = lax.rem(y + NY - dy, NY)
        await_bytes(slot_all.at[other], s_recv.at[dy])
        await_bytes(amp_all.at[other], y_recv.at[dy])
    group = BLK8 * CAP
    for q in range(NY):
        slot_of = slot_all[q, 0:1, :]
        here = slot_of == iota((NZ * group, ROWS), 0).astype(F32)
        lane = iota((NZ * group, ROWS), 1)
        rows = amp_all[q]
        for p in range(2):
            own = here & ((lane >= SL) if p else (lane < SL))
            part = dot(own.astype(F32).astype(BF16), rows).astype(BF16)
            slotted[:, pl.ds(q * group, group), pl.ds(p * V, V)] = part.reshape(NZ, group, V)

    for dx in range(1, NX):
        await_bytes(counts.at[lax.rem(x + NX - dx, NX)], n_recv.at[dx])
    n_out = NX * 4
    tall = iota((n_out * EB, NX * 16), 0) // EB
    pick_row = (iota((n_out * EB, NX * 16), 1) == (tall // 4) * 16 + lax.rem(tall, 4)).astype(F32).astype(BF16)
    tall_counts = dot(pick_row, counts[...].reshape(NX * 16, V)).astype(BF16)
    wide = iota((V, UNITS * EB), 1) // EB + x * UNITS
    pick_col = (iota((V, UNITS * EB), 0) == wide).astype(F32).astype(BF16)
    full = dot(tall_counts, pick_col)
    same = lax.rem(iota(full.shape, 0), EB) == lax.rem(iota(full.shape, 1), EB)
    spread[...] = jnp.where(same, full, 0.0).astype(BF16)

    await_bytes(blocks.at[:, :, 1 - c], core_recv.at[0])

    inter_acc[...] = jnp.zeros_like(inter_acc)
    lane_block = lax.rem(iota((SL, SLOTS), 1), group) // CAP

    def block_step(zz, carry):
        rows = slotted[zz]
        both_rows = rows[:, :V] + rows[:, V:]
        all_b = jnp.concatenate([blocks[k // NC, zz, k % NC] for k in range(BLK8)], axis=0)
        raw = dot_nt(all_b, both_rows)
        prod = jnp.zeros((SL, SLOTS), F32)
        for k in range(BLK8):
            prod = jnp.where(lane_block == k, raw[k * SL : (k + 1) * SL], prod)
        inter_acc[...] += dot(prod.astype(BF16), rows)
        return carry

    lax.fori_loop(0, NZ, block_step, 0)

    for p in range(2):
        inter[z, c, p] = inter_acc[:, pl.ds(p * V, V)].astype(BF16)

    def g_piece(zz, p, up, down):
        piece = inter.at[zz, c, p]
        if up is not None:

            @pl.when(up)
            def _():
                send_piece(piece, send_sem.at[6], g_recv.at[zz, p], z_up)

        if down is not None:

            @pl.when(down)
            def _():
                send_piece(piece, send_sem.at[6], g_recv.at[zz, p], z_down)

        send_piece(piece, send_sem.at[7], gc_recv.at[0], mate)

    for p in range(2):
        g_piece(z, p, True, True)

    def ring_step(s, carry):
        for p in range(2):
            zz = lax.rem(z - s + NZ, NZ)
            await_bytes(inter.at[zz, c, p], g_recv.at[zz, p])
            g_piece(zz, p, s < last, None)

            @pl.when(s < last)
            def _():
                zl = lax.rem(z + s, NZ)
                await_bytes(inter.at[zl, c, p], g_recv.at[zl, p])
                g_piece(zl, p, None, s < last - 1)

        return carry

    lax.fori_loop(1, last + 1, ring_step, 0)
    await_bytes(inter.at[:, 1 - c], gc_recv.at[0])

    low_lane = iota((EB, 128), 1) < SL

    def sum_step(eb, carry):
        at = pl.ds(pl.multiple_of(eb * EB, EB), EB)
        part = inter[:, :, :, at, :].reshape(UNITS * EB, V)
        sums = dot(spread[...], part)
        for xd in range(NX):
            for p in range(2):
                base = (xd * 4 + p * 2) * EB
                first, second = sums[base : base + EB], sums[base + EB : base + 2 * EB]
                for yd in range(NY):
                    t = (yd // 2) * 128
                    f, g = first[:, t : t + 128], second[:, t : t + 128]
                    if yd % 2 == 0:
                        joined = jnp.where(low_lane, f, pltpu.roll(g, SL, 1))
                    else:
                        joined = jnp.where(low_lane, pltpu.roll(f, SL, 1), g)
                    w_send[xd, yd, p, at, :] = joined.astype(BF16)
        return carry

    lax.fori_loop(0, SL // EB, sum_step, 0)

    for dx, dy in offsets:
        there = at_xy(dx, dy)
        remote(
            w_send.at[there["pairs_0"], there["ints"]],
            w_recv.at[dx, dy],
            send_sem.at[8 if dx else 10],
            w_rsem.at[dx, dy],
            there,
        ).start()
    w_recv[0, 0] = w_send[x, y]
    for dx, dy in offsets:
        await_bytes(w_recv.at[dx, dy], w_rsem.at[dx, dy])

    lane_low = iota((SL, 128), 1) < SL
    for p in range(2):
        parts = []
        for q in range(NY):
            dy = lax.rem(y - q + NY, NY)
            parts.append(sum(w_recv[dx, dy, p].astype(F32) for dx in range(NX)))
        w = jnp.transpose(jnp.concatenate(parts, axis=0)).astype(BF16)
        cycle = jnp.zeros((SL, V), F32)
        for j in range(2):
            rows = amp_all[:, pl.ds(j * SL, SL), :].reshape(V, V)
            cycle += dot(w[j * SL : (j + 1) * SL], rows)
        mine_rows = ecol_ref[p, pl.ds(pl.multiple_of(y * SL, SL), SL), :]
        scaled[p] = (resid_ref[p] + cycle) / (mine_rows + erow_ref[p])
    for q in range(NY):
        t = (q // 2) * 128
        f, g = scaled[0, :, pl.ds(t, 128)], scaled[1, :, pl.ds(t, 128)]
        if q % 2 == 0:
            joined = jnp.where(lane_low, f, pltpu.roll(g, SL, 1))
        else:
            joined = jnp.where(lane_low, pltpu.roll(f, SL, 1), g)
        m_send[q] = joined.astype(BF16)
    for dy in range(NY):
        there = at_xy(NX // 2, dy)
        remote(m_send.at[there["ints"]], m_recv.at[dy], send_sem.at[9], m_rsem.at[dy], there).start()
    for dy in range(NY):
        await_bytes(m_recv.at[dy], m_rsem.at[dy])
    mirror = jnp.concatenate([m_recv[lax.rem(y - q + NY, NY)].astype(F32) for q in range(NY)], axis=0)
    mirror = jnp.transpose(mirror)
    for p in range(2):
        other = jnp.where(swap_ref[p] > 0.5, mirror[SL:], mirror[:SL])
        out_ref[p] = -0.5 * (scaled[p] + other)

    await_bytes(blocks.at[0, pl.ds(0, NZ - 1), 0], send_sem.at[0])
    await_bytes(blocks.at[pl.ds(0, NX - 1), :, 0], send_sem.at[1])
    await_bytes(blocks.at[:, :, 0], send_sem.at[2])
    await_bytes(slot_all.at[pl.ds(0, NY - 1)], send_sem.at[3])
    await_bytes(amp_all.at[pl.ds(0, NY - 1)], send_sem.at[4])
    await_bytes(counts.at[pl.ds(0, NX - 1)], send_sem.at[5])
    await_bytes(inter.at[pl.ds(0, NZ - 1), 0], send_sem.at[6])
    await_bytes(inter.at[:, 0], send_sem.at[7])
    await_bytes(w_recv.at[pl.ds(0, NX - 1)], send_sem.at[8])
    await_bytes(w_recv.at[0, pl.ds(0, NY - 1)], send_sem.at[10])
    await_bytes(m_recv.at[:], send_sem.at[9])


def body(
    amps,
    resid_rest,
    int_blocks,
    virt_energy,
    pair_energy,
    item_block,
    share_owner,
    share_pair,
    share_amp,
    transpose_pair,
):
    n_pairs = lax.axis_size(PAIRS)
    pair_index = lax.axis_index(PAIRS)
    partner = (pair_index + n_pairs // 2) % n_pairs
    swap = (transpose_pair - partner * 2).astype(F32).reshape(2, 1, 1)
    row_block = jnp.repeat(item_block[:, 0], 2)
    unit = share_owner * 2 + share_pair
    rows_energy = (virt_energy - pair_energy[:, None])[:, :, None]
    vmem = pl.BlockSpec(memory_space=pltpu.VMEM)
    dma = pltpu.SemaphoreType.DMA
    return pl.pallas_call(
        kernel,
        out_shape=jax.ShapeDtypeStruct((2, SL, V), F32),
        in_specs=[vmem] * 10,
        out_specs=vmem,
        scratch_shapes=[
            pltpu.VMEM((V, V), F32),
            pltpu.VMEM((NX, NZ, NC, SL, V), BF16),
            pltpu.VMEM((NY, ROWS, V), BF16),
            pltpu.VMEM((NY, 8, ROWS), F32),
            pltpu.VMEM((NX, 16, V), BF16),
            pltpu.VMEM((NX * 4 * EB, UNITS * EB), BF16),
            pltpu.VMEM((NZ, SLOTS, 2 * V), BF16),
            pltpu.VMEM((SL, 2 * V), F32),
            pltpu.VMEM((NZ, NC, 2, SL, V), BF16),
            pltpu.VMEM((NX, NY, 2, SL, 128), BF16),
            pltpu.VMEM((NX, NY, 2, SL, 128), BF16),
            pltpu.VMEM((2, SL, V), F32),
            pltpu.VMEM((NY, SL, 128), BF16),
            pltpu.VMEM((NY, SL, 128), BF16),
            dma((11,)),
            dma((NY,)),
            dma((NY,)),
            dma((NX,)),
            dma((NZ,)),
            dma((2, NZ)),
            dma((2, NZ)),
            dma((1,)),
            dma((NZ, 2)),
            dma((1,)),
            dma((NX, NY)),
            dma((NY,)),
        ],
        compiler_params=pltpu.CompilerParams(collective_id=0, has_side_effects=True),
        name="cycle",
    )(
        amps.reshape(ROWS, V),
        resid_rest,
        int_blocks[0],
        rows_energy,
        virt_energy[:, None, :],
        row_block[:, None],
        row_block[None, :],
        unit,
        share_amp.reshape(1, -1),
        swap,
    )


def solution(mesh):
    torus = Mesh(
        mesh.devices.reshape(NX, NZ, NC, mesh.shape["ints"]),
        ("pairs_0", "pairs_1", "pairs_2", "ints"),
    )
    return jax.shard_map(
        body,
        mesh=torus,
        in_specs=(
            P(PAIRS, "ints", None),
            P(PAIRS, "ints", None),
            P(PAIRS, None, None),
            P(PAIRS, None),
            P(PAIRS),
            P(PAIRS_INTS, None),
            P(PAIRS, None),
            P(PAIRS, None),
            P(PAIRS, None),
            P(PAIRS),
        ),
        out_specs=P(PAIRS, "ints", None),
        check_vma=False,
    )
```

time: 274 us -> 108 us (0.39)
  waiting for transfers between devices: 119 us -> 0 us
  Pallas kernels: 0 us -> 100 us
  blocking collectives: 72.3 us -> 0 us
  local copies, waits for them, and re-layouts: 31.4 us -> 7.26 us
  starting transfers between devices: 14.4 us -> 0 us
  between operations: 13.7 us -> 0.02 us
  other arithmetic: 11 us -> 0.08 us
  matrix products: 9.72 us -> 0 us
    pallas_call x0 -> x1, Pallas kernels: none -> 100 us  [body(): pl.pallas_call(kernel, out_shape=jax.ShapeDtypeStruct((2, SL, V), F32), i...]
    all_gather x2 -> x0, waiting for transfers between devices: 90.3 us -> none  [stacked_from(): tiles = lax.all_gather(tiles, axes[k])]
    all_to_all x2 -> x0, blocking collectives: 52.1 us -> none  [the longest x1 42.6 us: body(): lax.all_to_all(outgoing, PAIRS, split_axis=0, concat_axis=0, tiled=True)]
    all_to_all x2 -> x0, waiting for transfers between devices: 26.9 us -> none  [the longest x1 22.4 us: body(): lax.all_to_all(product, PAIRS, split_axis=0, concat_axis=0, tiled=True)]
    all_gather x2 -> x0, blocking collectives: 20.3 us -> none  [the longest x1 10.1 us: body(): amp_full = lax.all_gather(amp_half, 'ints', axis=1, tiled=True)]
    gather x5 -> x0, local copies, waits for them, and re-layouts: 16.8 us -> none  [the longest x2 9.6 us: cycle_one(): amp_full[amp_index]]
    all_to_all x2 -> x0, starting transfers between devices: 10.6 us -> none  [the longest x1 7.35 us: body(): lax.all_to_all(product, PAIRS, split_axis=0, concat_axis=0, tiled=True)]
    dot_general x4 -> x0, matrix products: 9.72 us -> none  [the longest x2 9.22 us: cycle_one(): jnp.einsum('kac,kcb->ab', w_req, amp_full[amp_index], preferred_element_t...]
  transfers between devices with their start and end apart: 5 -> 0, of which waited for: 5 -> 0; matrix products, arithmetic and copies ran while one was open for 1% -> 0% of each run, Pallas kernels for 0% -> 0%
where the time goes in v1:
time: 108 us; the launch traced here: 107 us
  Pallas kernels  100 us (93%)
  local copies, waits for them, and re-layouts  7.26 us (7%)
    pallas_call x1, Pallas kernels, body(): pl.pallas_call(kernel, out_shape=jax.ShapeDtypeStruct((2, SL, V), F32), i...  100 us
    unnamed x13, local copies, waits for them, and re-layouts  2.98 us

profile of v1, /device:TPU:1, one launch (start us, length us, event | category | flops | bytes accessed | tf_op | source)
XLA Modules:
  0.0 107.4 jit_solution(6092025239177506678)
XLA Ops:
  0.0 0.0 copy-start.3
  0.0 0.7 copy-done.3
  0.7 0.0 copy-start.4
  0.7 0.0 copy-start.5
  0.7 0.7 copy-done.4
  1.3 0.0 copy-done.5
  1.3 0.0 copy-start
  1.3 0.0 copy-start.2
  1.3 0.7 copy.25.swap_ref
  2.0 0.0 copy-done
  2.0 0.0 copy-done.2
  2.0 0.1 subtract_bitcast_fusion
  2.1 0.0 copy-start.1
  2.1 0.6 broadcast_in_dim.11.erow_ref
  2.7 0.1 copy-done.1
  2.7 0.1 broadcast_in_dim.12
  2.8 0.7 broadcast_in_dim_reshape.7.brow_ref
  3.5 0.7 broadcast_in_dim_reshape.8.bcol_ref
  4.2 0.7 copy.24.unit_ref
  4.9 0.9 copy.22.ecol_ref
  5.8 100.0 %cycle.1 = f32[2,64,256]{2,1,0:T(8,128)} custom-call(f32[128,256]{1,0:T(8,128)} %bitcast.8, f32[2,64,256]{2,1,0:T(8,128)} %resid_ref.1, bf16[256,256]{1,0:T(8,128)(2,1)} %bitcast.9, f32[2,256,1]{2,1,0:T(8,128)} %copy.22.ecol_ref, f32[2,1,256]{2,1,0:T(1,128)} %broadcast_in_dim.11.erow_ref, s32[128,1]{1,0:T(8,128)} %broadcast_in_dim_reshape.8.bcol_ref, ...), custom_call_target="tpu_custom_call" | custom-call | tf_op jit(solution)/shard_map/cycle/pallas_call | solution.py:387
  105.8 1.6 %copy.27 = f32[2,64,256]{2,1,0:T(8,128)} copy(f32[2,64,256]{2,1,0:T(8,128)} %cycle.1) | data formatting | bytes 262144
  (2 shorter events, 0.0 us)
Async XLA Ops:
  0.0 0.7 copy-start.3
  0.7 0.7 copy-start.4
  0.7 0.7 copy-start.5
  1.3 0.7 copy-start
  1.3 0.7 copy-start.2
  2.1 0.7 copy-start.1

commit v2 on v1

v2 whole, which is shorter than its diff:
```python
import functools

import jax
import jax.numpy as jnp
from jax import lax
from jax.experimental import pallas as pl
from jax.experimental.pallas import tpu as pltpu
from jax.sharding import Mesh
from jax.sharding import PartitionSpec as P

PAIRS = ("pairs_0", "pairs_1", "pairs_2")
PAIRS_INTS = ("pairs_0", "pairs_1", "pairs_2", "ints")
MESH = pl.DeviceIdType.MESH
F32 = jnp.float32
BF16 = jnp.bfloat16
NX, NZ, NC, NY = 4, 16, 2, 4
V = 256
SL = V // NY
ROWS = 2 * SL
HALF = SL // 2
CAP = 4
BLK8 = NX * NC
SLOTS = NY * BLK8 * CAP
UNITS = NZ * NC * 2
EB = 16
N_EB = SL // EB
BLOCK_PLAN = {0: (4, 2, 1), 2: (1,), 4: (4, 2, 1), 6: (1,)}
BLOCK_TIME = {1: 3.5, 2: 4.5, 4: 5.5, 3: 8.0, 5: 10.0, 6: 11.0, 7: 14.0, 8: 15.0}
RING_PLAN = {0: (4, 1), 1: (1,), 2: (1,), 4: (1,), 5: (1,), 6: (1,), 7: (1,)}
RING_TIME = {1: 2.4, 4: 4.2, 2: 4.8, 5: 6.6, 3: 7.2, 6: 9.0, 7: 11.4, 8: 13.8}


def sends_of(plan, offset):
    half = NZ // 2
    up = [k for k in plan.get(offset, ()) if offset >= 0 and offset + k <= half]
    down = [-k for k in plan.get(-offset, ()) if offset <= 0 and k - offset < half]
    return [k for pair in zip(up, down) for k in pair] if offset == 0 else up + down


def gather_events():
    pieces = [(0.0, 0)] + [(t, o) for o, t in BLOCK_TIME.items()] + [(t, -o) for o, t in BLOCK_TIME.items() if o < NZ // 2]
    pieces.sort()
    events = [(6.0, 5, 0, "slots"), (7.0, 5, 0, "spread")]
    near = far = 0.0
    for t, o in pieces:
        near = max(near + 0.9, t + 2.8)
        far = max(far + 1.0, near + 2.8)
        if o:
            events.append((t, 0, o, "z"))
        events += [(near, 1, o, "x"), (far, 2, o, "far"), (far + 2.0, 3, o, "work")]
    return [(kind, o) for _, _, o, kind in sorted(events)]


def iota(shape, dim):
    return lax.broadcasted_iota(jnp.int32, shape, dim)


def dot_nt(a, b):
    return lax.dot_general(a, b, (((1,), (1,)), ((), ())), preferred_element_type=F32)


def dot(a, b):
    return jnp.dot(a, b, preferred_element_type=F32)


def ring_events():
    events = []
    for eb in range(N_EB):
        events.append((1.5 * eb, eb, 0, "ring"))
        for o, t in RING_TIME.items():
            for signed in (o, -o) if o < NZ // 2 else (o,):
                events.append((t + eb + 1.0, eb, signed, "ring"))
        events.append((RING_TIME[NZ // 2] + eb + 3.0, eb, 0, "sum"))
    return [(kind, o, eb) for _, eb, o, kind in sorted(events)]


def kernel(
    amps_hbm,
    resid_hbm,
    block_hbm,
    energy_hbm,
    item_hbm,
    owner_hbm,
    pair_hbm,
    mate_hbm,
    pair_energy_hbm,
    twin_hbm,
    out_ref,
    turned,
    blocks,
    amp_all,
    slot_all,
    counts,
    spread,
    slotted,
    inter_acc,
    inter,
    w_send,
    w_recv,
    scaled,
    m_send,
    m_recv,
    ecol,
    amps_ref,
    resid,
    block_ref,
    energy_ref,
    item_ref,
    owner_ref,
    pair_ref,
    mate_ref,
    pair_energy_ref,
    twin_ref,
    local_sem,
    send_sem,
    y_recv,
    s_recv,
    n_recv,
    z_recv,
    xw_recv,
    xh_recv,
    core_recv,
    g_recv,
    gc_recv,
    w_rsem,
    m_rsem,
):
    x = lax.axis_index("pairs_0")
    z = lax.axis_index("pairs_1")
    c = lax.axis_index("pairs_2")
    y = lax.axis_index("ints")
    mate = {"pairs_2": 1 - c}
    x_up = {"pairs_0": lax.rem(x + 1, NX)}
    x_down = {"pairs_0": lax.rem(x + NX - 1, NX)}

    def at_z(k):
        return {"pairs_1": lax.rem(z + k + NZ, NZ)}

    def at_xy(dx, dy):
        return {"pairs_0": lax.rem(x + dx, NX), "ints": lax.rem(y + dy, NY)}

    def remote(src, dst, ssem, rsem, device):
        return pltpu.make_async_remote_copy(
            src_ref=src, dst_ref=dst, send_sem=ssem, recv_sem=rsem, device_id=device, device_id_type=MESH
        )

    def await_bytes(ref, sem):
        pltpu.make_async_copy(ref, ref, sem).wait()

    held = (amps_hbm, resid_hbm, block_hbm, energy_hbm, item_hbm, owner_hbm, pair_hbm, mate_hbm, pair_energy_hbm, twin_hbm)
    used = (amps_ref, resid, block_ref, energy_ref, item_ref, owner_ref, pair_ref, mate_ref, pair_energy_ref, twin_ref)
    copies = [pltpu.make_async_copy(a, b, local_sem.at[i]) for i, (a, b) in enumerate(zip(held, used))]
    for i in (2, 0, 4, 5, 6, 7, 3, 8, 9, 1):
        copies[i].start()

    barrier = pltpu.get_barrier_semaphore()
    offsets = [(dx, dy) for dx in range(NX) for dy in range(NY) if dx or dy]
    z_steps = sorted({k for plan in (BLOCK_PLAN, RING_PLAN) for steps in plan.values() for k in steps})
    greeted = [at_z(k) for step in z_steps for k in (step, -step)] + [mate] + [at_xy(dx, dy) for dx, dy in offsets]
    for device in greeted:
        pl.semaphore_signal(barrier, inc=1, device_id=device, device_id_type=MESH)

    copies[2].wait()
    turned[...] = jnp.transpose(block_ref[...].astype(F32))
    blocks[x, z, c] = turned[pl.ds(pl.multiple_of(y * SL, SL), SL), :].astype(BF16)
    copies[0].wait()
    amp_all[y] = amps_ref[...].astype(BF16)

    copies[4].wait()
    n_items = item_ref.shape[1]
    twice = (iota((n_items, ROWS), 0) == iota((n_items, ROWS), 1) // 2).astype(F32).astype(BF16)
    item = jnp.broadcast_to(item_ref[...].astype(F32), (16, n_items)).astype(BF16)
    row = dot(item, twice)[0:1].astype(jnp.int32)
    square = jnp.broadcast_to(row, (ROWS, ROWS)).astype(F32)
    earlier = (jnp.transpose(square) == square) & (iota((ROWS, ROWS), 0) < iota((ROWS, ROWS), 1))
    rank = jnp.sum(earlier.astype(F32), axis=0, keepdims=True)
    z_of = (row >> 1) & (NZ - 1)
    place = z_of * (BLK8 * CAP) + ((row >> 5) * NC + (row & 1)) * CAP
    slot_all[y] = jnp.broadcast_to(place.astype(F32) + rank, (8, ROWS))

    for i in (5, 6, 7):
        copies[i].wait()
    n_req = owner_ref.shape[1]
    unit = owner_ref[...] * 2 + pair_ref[...]
    hot = (iota((V, n_req), 0) == unit).astype(F32).astype(BF16)
    out_id = iota((16, n_req), 0)
    mine = (iota((16, n_req), 1) // (n_req // 2)) * 2 + mate_ref[...]
    pick = (out_id == mine).astype(F32).astype(BF16)
    counts[x] = dot_nt(pick, hot).astype(BF16)

    pl.semaphore_wait(barrier, len(greeted))

    def send_piece(ref, ssem, rsem, device):
        remote(ref, ref, ssem, rsem, device).start()

    def z_of_piece(o):
        return lax.rem(z - o + NZ, NZ)

    def z_piece(o):
        zz = z_of_piece(o)
        piece = blocks.at[x, zz, c]
        if o:
            await_bytes(piece, z_recv.at[zz])
        for k in sends_of(BLOCK_PLAN, o):
            send_piece(piece, send_sem.at[0], z_recv.at[zz], at_z(k))
        send_piece(piece, send_sem.at[1], xw_recv.at[0, zz], x_up)
        send_piece(piece, send_sem.at[1], xw_recv.at[1, zz], x_down)
        send_piece(piece, send_sem.at[2], core_recv.at[zz], mate)

    xl, xr, xo = lax.rem(x + NX - 1, NX), lax.rem(x + 1, NX), lax.rem(x + 2, NX)

    def x_piece(o):
        zz = z_of_piece(o)
        await_bytes(blocks.at[xl, zz, c], xw_recv.at[0, zz])
        low = blocks.at[xl, zz, c, pl.ds(0, HALF), :]
        send_piece(low, send_sem.at[1], xh_recv.at[0, zz], x_up)
        send_piece(blocks.at[xl, zz, c], send_sem.at[2], core_recv.at[zz], mate)
        await_bytes(blocks.at[xr, zz, c], xw_recv.at[1, zz])
        high = blocks.at[xr, zz, c, pl.ds(HALF, HALF), :]
        send_piece(high, send_sem.at[1], xh_recv.at[1, zz], x_down)
        send_piece(blocks.at[xr, zz, c], send_sem.at[2], core_recv.at[zz], mate)

    def far_piece(o):
        zz = z_of_piece(o)
        await_bytes(blocks.at[xo, zz, c, pl.ds(0, HALF), :], xh_recv.at[0, zz])
        await_bytes(blocks.at[xo, zz, c, pl.ds(HALF, HALF), :], xh_recv.at[1, zz])
        send_piece(blocks.at[xo, zz, c], send_sem.at[2], core_recv.at[zz], mate)

    group = BLK8 * CAP

    def slot_rows():
        for dy in range(1, NY):
            other = lax.rem(y + NY - dy, NY)
            await_bytes(slot_all.at[other], s_recv.at[dy])
            await_bytes(amp_all.at[other], y_recv.at[dy])
        for q in range(NY):
            slot_of = slot_all[q, 0:1, :]
            here = slot_of == iota((NZ * group, ROWS), 0).astype(F32)
            lane = iota((NZ * group, ROWS), 1)
            rows = amp_all[q]
            for p in range(2):
                own = here & ((lane >= SL) if p else (lane < SL))
                part = dot(own.astype(F32).astype(BF16), rows).astype(BF16)
                slotted[:, pl.ds(q * group, group), pl.ds(p * V, V)] = part.reshape(NZ, group, V)

    def spread_counts():
        for dx in range(1, NX):
            await_bytes(counts.at[lax.rem(x + NX - dx, NX)], n_recv.at[dx])
        n_out = NX * 4
        tall = iota((n_out * EB, NX * 16), 0) // EB
        pick_row = (iota((n_out * EB, NX * 16), 1) == (tall // 4) * 16 + lax.rem(tall, 4)).astype(F32).astype(BF16)
        tall_counts = dot(pick_row, counts[...].reshape(NX * 16, V)).astype(BF16)
        wide = iota((V, UNITS * EB), 1) // EB + x * UNITS
        pick_col = (iota((V, UNITS * EB), 0) == wide).astype(F32).astype(BF16)
        full = dot(tall_counts, pick_col)
        same = lax.rem(iota(full.shape, 0), EB) == lax.rem(iota(full.shape, 1), EB)
        spread[...] = jnp.where(same, full, 0.0).astype(BF16)
        copies[3].wait()
        for p in range(2):
            ecol[p] = jnp.transpose(jnp.broadcast_to(energy_ref[p : p + 1, :], (128, V)))

    lane_block = lax.rem(iota((SL, SLOTS), 1), group) // CAP

    def block_work(o):
        zz = z_of_piece(o)
        await_bytes(blocks.at[:, zz, 1 - c], core_recv.at[zz])
        rows = slotted[zz]
        both_rows = rows[:, :V] + rows[:, V:]
        all_b = jnp.concatenate([blocks[k // NC, zz, k % NC] for k in range(BLK8)], axis=0)
        raw = dot_nt(all_b, both_rows)
        prod = jnp.zeros((SL, SLOTS), F32)
        for k in range(BLK8):
            prod = jnp.where(lane_block == k, raw[k * SL : (k + 1) * SL], prod)
        inter_acc[...] += dot(prod.astype(BF16), rows)

    z_piece(0)
    for dy in range(1, NY):
        send_piece(slot_all.at[y], send_sem.at[3], s_recv.at[dy], at_xy(0, dy))
        send_piece(amp_all.at[y], send_sem.at[4], y_recv.at[dy], at_xy(0, dy))
    for dx in range(1, NX):
        send_piece(counts.at[x], send_sem.at[5], n_recv.at[dx], at_xy(dx, 0))
    inter_acc[...] = jnp.zeros_like(inter_acc)

    for kind, o in gather_events():
        if kind == "slots":
            slot_rows()
        elif kind == "spread":
            spread_counts()
        else:
            {"z": z_piece, "x": x_piece, "far": far_piece, "work": block_work}[kind](o)

    for eb in range(N_EB):
        for p in range(2):
            inter[eb, z, c, p] = inter_acc[pl.ds(eb * EB, EB), pl.ds(p * V, V)].astype(BF16)

    def ring_piece(o, eb):
        zz = z_of_piece(o)
        piece = inter.at[eb, zz, c]
        if o:
            await_bytes(piece, g_recv.at[eb, zz])
        for k in sends_of(RING_PLAN, o):
            send_piece(piece, send_sem.at[6], g_recv.at[eb, zz], at_z(k))
        send_piece(piece, send_sem.at[7], gc_recv.at[eb], mate)

    low_lane = iota((EB, 128), 1) < SL

    def sum_part(eb):
        await_bytes(inter.at[eb, :, 1 - c], gc_recv.at[eb])
        part = inter[eb].reshape(UNITS * EB, V)
        sums = dot(spread[...], part)
        for xd in range(NX):
            for p in range(2):
                base = (xd * 4 + p * 2) * EB
                first, second = sums[base : base + EB], sums[base + EB : base + 2 * EB]
                for yd in range(NY):
                    t = (yd // 2) * 128
                    f, g = first[:, t : t + 128], second[:, t : t + 128]
                    if yd % 2 == 0:
                        joined = jnp.where(low_lane, f, pltpu.roll(g, SL, 1))
                    else:
                        joined = jnp.where(low_lane, pltpu.roll(f, SL, 1), g)
                    w_send[xd, yd, eb, p] = joined.astype(BF16)
        for dx, dy in offsets:
            there = at_xy(dx, dy)
            remote(
                w_send.at[there["pairs_0"], there["ints"], eb],
                w_recv.at[dx, dy, eb],
                send_sem.at[8 if dx else 10],
                w_rsem.at[dx, dy],
                there,
            ).start()

    for kind, o, eb in ring_events():
        if kind == "ring":
            ring_piece(o, eb)
        else:
            sum_part(eb)

    w_recv[0, 0] = w_send[x, y]
    for i in (1, 8, 9):
        copies[i].wait()
    for dx, dy in offsets:
        await_bytes(w_recv.at[dx, dy], w_rsem.at[dx, dy])

    lane_low = iota((SL, 128), 1) < SL
    for p in range(2):
        parts = []
        for q in range(NY):
            dy = lax.rem(y - q + NY, NY)
            for eb in range(N_EB):
                parts.append(sum(w_recv[dx, dy, eb, p].astype(F32) for dx in range(NX)))
        w = jnp.transpose(jnp.concatenate(parts, axis=0)).astype(BF16)
        cycle = jnp.zeros((SL, V), F32)
        for j in range(2):
            rows = amp_all[:, pl.ds(j * SL, SL), :].reshape(V, V)
            cycle += dot(w[j * SL : (j + 1) * SL], rows)
        mine_rows = ecol[p, pl.ds(pl.multiple_of(y * SL, SL), SL), :]
        mine_rows = jnp.concatenate([mine_rows, mine_rows], axis=1)
        divisor = mine_rows + energy_ref[p : p + 1, :] - pair_energy_ref[p]
        scaled[p] = (resid[p] + cycle) / divisor
    for q in range(NY):
        t = (q // 2) * 128
        f, g = scaled[0, :, pl.ds(t, 128)], scaled[1, :, pl.ds(t, 128)]
        if q % 2 == 0:
            joined = jnp.where(lane_low, f, pltpu.roll(g, SL, 1))
        else:
            joined = jnp.where(lane_low, pltpu.roll(f, SL, 1), g)
        m_send[q] = joined.astype(BF16)
    for dy in range(NY):
        there = at_xy(NX // 2, dy)
        remote(m_send.at[there["ints"]], m_recv.at[dy], send_sem.at[9], m_rsem.at[dy], there).start()
    for dy in range(NY):
        await_bytes(m_recv.at[dy], m_rsem.at[dy])
    mirror = jnp.concatenate([m_recv[lax.rem(y - q + NY, NY)].astype(F32) for q in range(NY)], axis=0)
    mirror = jnp.transpose(mirror)
    first_twin = ((xo * NZ + z) * NC + c) * 2
    for p in range(2):
        which = jnp.full((SL, V), twin_ref[p] - first_twin)
        other = jnp.where(which == 1, mirror[SL:], mirror[:SL])
        out_ref[p] = -0.5 * (scaled[p] + other)

    await_bytes(blocks.at[0, pl.ds(0, NZ - 1), 0], send_sem.at[0])
    await_bytes(blocks.at[pl.ds(0, NX - 1), :, 0], send_sem.at[1])
    await_bytes(blocks.at[:, :, 0], send_sem.at[2])
    await_bytes(slot_all.at[pl.ds(0, NY - 1)], send_sem.at[3])
    await_bytes(amp_all.at[pl.ds(0, NY - 1)], send_sem.at[4])
    await_bytes(counts.at[pl.ds(0, NX - 1)], send_sem.at[5])
    await_bytes(inter.at[:, pl.ds(0, NZ - 1), 0], send_sem.at[6])
    await_bytes(inter.at[:, :, 0], send_sem.at[7])
    await_bytes(w_recv.at[pl.ds(0, NX - 1)], send_sem.at[8])
    await_bytes(w_recv.at[0, pl.ds(0, NY - 1)], send_sem.at[10])
    await_bytes(m_recv.at[:], send_sem.at[9])


def body(
    amps,
    resid_rest,
    int_blocks,
    virt_energy,
    pair_energy,
    item_block,
    share_owner,
    share_pair,
    share_amp,
    transpose_pair,
):
    n_items, n_req = item_block.shape[0], share_owner.shape[0]
    dma = pltpu.SemaphoreType.DMA
    return pl.pallas_call(
        kernel,
        out_shape=jax.ShapeDtypeStruct((2, SL, V), F32),
        in_specs=[pl.BlockSpec(memory_space=pl.ANY)] * 10,
        out_specs=pl.BlockSpec(memory_space=pltpu.VMEM),
        scratch_shapes=[
            pltpu.VMEM((V, V), F32),
            pltpu.VMEM((NX, NZ, NC, SL, V), BF16),
            pltpu.VMEM((NY, ROWS, V), BF16),
            pltpu.VMEM((NY, 8, ROWS), F32),
            pltpu.VMEM((NX, 16, V), BF16),
            pltpu.VMEM((NX * 4 * EB, UNITS * EB), BF16),
            pltpu.VMEM((NZ, SLOTS, 2 * V), BF16),
            pltpu.VMEM((SL, 2 * V), F32),
            pltpu.VMEM((N_EB, NZ, NC, 2, EB, V), BF16),
            pltpu.VMEM((NX, NY, N_EB, 2, EB, 128), BF16),
            pltpu.VMEM((NX, NY, N_EB, 2, EB, 128), BF16),
            pltpu.VMEM((2, SL, V), F32),
            pltpu.VMEM((NY, SL, 128), BF16),
            pltpu.VMEM((NY, SL, 128), BF16),
            pltpu.VMEM((2, V, 128), F32),
            pltpu.VMEM((ROWS, V), F32),
            pltpu.VMEM((2, SL, V), F32),
            pltpu.VMEM((V, V), BF16),
            pltpu.VMEM((2, V), F32),
            pltpu.VMEM((1, n_items), jnp.int32),
            pltpu.VMEM((1, n_req), jnp.int32),
            pltpu.VMEM((1, n_req), jnp.int32),
            pltpu.VMEM((1, n_req), jnp.int32),
            pltpu.SMEM((2,), F32),
            pltpu.SMEM((2,), jnp.int32),
            dma((10,)),
            dma((11,)),
            dma((NY,)),
            dma((NY,)),
            dma((NX,)),
            dma((NZ,)),
            dma((2, NZ)),
            dma((2, NZ)),
            dma((NZ,)),
            dma((N_EB, NZ)),
            dma((N_EB,)),
            dma((NX, NY)),
            dma((NY,)),
        ],
        compiler_params=pltpu.CompilerParams(collective_id=0, has_side_effects=True),
        name="cycle",
    )(
        amps.reshape(ROWS, V),
        resid_rest,
        int_blocks[0],
        virt_energy,
        item_block.reshape(1, -1),
        share_owner.reshape(1, -1),
        share_pair.reshape(1, -1),
        share_amp.reshape(1, -1),
        pair_energy,
        transpose_pair,
    )


def solution(mesh):
    torus = Mesh(
        mesh.devices.reshape(NX, NZ, NC, mesh.shape["ints"]),
        ("pairs_0", "pairs_1", "pairs_2", "ints"),
    )
    return jax.shard_map(
        body,
        mesh=torus,
        in_specs=(
            P(PAIRS, "ints", None),
            P(PAIRS, "ints", None),
            P(PAIRS, None, None),
            P(PAIRS, None),
            P(PAIRS),
            P(PAIRS_INTS, None),
            P(PAIRS, None),
            P(PAIRS, None),
            P(PAIRS, None),
            P(PAIRS),
        ),
        out_specs=P(PAIRS, "ints", None),
        check_vma=False,
    )
```

time: 108 us -> 85.1 us (0.79)
  Pallas kernels: 100 us -> 83.4 us
  local copies, waits for them, and re-layouts: 7.26 us -> 1.57 us
    pallas_call x1, Pallas kernels: 100 us -> 83.4 us  [body(): pl.pallas_call(kernel, out_shape=jax.ShapeDtypeStruct((2, SL, V), F32), i...]
    broadcast_in_dim x3 -> x0, local copies, waits for them, and re-layouts: 1.51 us -> none  [the longest x1 0.85 us: body(): rows_energy = (virt_energy - pair_energy[:, None])[:, :, None]]
    unnamed x13 -> x1, local copies, waits for them, and re-layouts: 2.98 us -> 1.57 us
    another operation x2 -> x0, local copies, waits for them, and re-layouts: 1.39 us -> none  [the longest x1 0.7 us: body(): row_block[:, None]]
where the time goes in v2:
time: 85.1 us; the launch traced here: 84.9 us
  Pallas kernels  83.4 us (98%)
  local copies, waits for them, and re-layouts  1.57 us (2%)
    pallas_call x1, Pallas kernels, body(): pl.pallas_call(kernel, out_shape=jax.ShapeDtypeStruct((2, SL, V), F32), i...  83.4 us

profile of v2, /device:TPU:1, one launch (start us, length us, event | category | flops | bytes accessed | tf_op | source)
XLA Modules:
  0.0 84.9 jit_solution(17961757929794951727)
XLA Ops:
  0.0 83.4 %cycle.1 = f32[2,64,256]{2,1,0:T(8,128)} custom-call(f32[128,256]{1,0:T(8,128)} %bitcast.6, f32[2,64,256]{2,1,0:T(8,128)} %resid_hbm.1, bf16[256,256]{1,0:T(8,128)(2,1)} %bitcast.7, f32[2,256]{1,0:T(2,128)} %energy_hbm.1, s32[1,64]{1,0:T(1,128)} %bitcast.8, s32[1,96]{1,0:T(1,128)} %bitcast.9, s32[1,96]{1,0:T(1,128)} %bitcast.10, s32[1,96]{1,0:T(1,128)} %bitcast.11, ...), custom_call_target="tpu_custom_call" | custom-call | tf_op jit(solution)/shard_map/cycle/pallas_call | solution.py:409
  83.4 1.6 %copy.12 = f32[2,64,256]{2,1,0:T(8,128)} copy(f32[2,64,256]{2,1,0:T(8,128)} %cycle.1) | data formatting | bytes 262144

commit v3 on v2

--- a/solution.py
+++ b/solution.py
@@ -24,10 +24,36 @@
 UNITS = NZ * NC * 2
 EB = 16
 N_EB = SL // EB
-BLOCK_PLAN = {0: (4, 2, 1), 2: (1,), 4: (4, 2, 1), 6: (1,)}
-BLOCK_TIME = {1: 3.5, 2: 4.5, 4: 5.5, 3: 8.0, 5: 10.0, 6: 11.0, 7: 14.0, 8: 15.0}
-RING_PLAN = {0: (4, 1), 1: (1,), 2: (1,), 4: (1,), 5: (1,), 6: (1,), 7: (1,)}
-RING_TIME = {1: 2.4, 4: 4.2, 2: 4.8, 5: 6.6, 3: 7.2, 6: 9.0, 7: 11.4, 8: 13.8}
+FIRST = 16
+REST = SL - FIRST
+BLOCK_PLAN = {0: (1, 3), 1: (1,), 3: (1, 3), 4: (1,), 6: (1, 2)}
+FIRST_PLAN = {0: (1,), 1: (3, 1), 2: (1,), 3: (2,), 4: (2,), 6: (2, 1)}
+RING_PLAN = {0: (3, 1), 1: (1,), 3: (1,), 4: (2, 1), 6: (2, 1)}
+GATHER_ORDER = (
+    ("z", -1), ("z", 1), ("x", 0), ("first", 0), ("z", 3), ("z", -3), ("slots", 0), ("z", 2), ("z", -2),
+    ("spread", 0), ("x", 1), ("first", -1), ("first", 1), ("x", -1), ("far", 0), ("z", -4), ("z", 4), ("x", 3),
+    ("work", 0), ("x", -3), ("x", 2), ("x", -2), ("z", -6), ("z", 6), ("far", 1), ("far", -1), ("first", 2),
+    ("first", -2), ("x", -4), ("x", 4), ("work", 1), ("far", 3), ("far", -3), ("work", -1), ("z", -5), ("far", 2),
+    ("z", 5), ("first", 4), ("x", -6), ("first", -4), ("x", 6), ("z", -7), ("z", 7), ("far", -2), ("far", -4),
+    ("work", 2), ("first", -3), ("first", 3), ("far", 4), ("work", -2), ("z", 8), ("work", -4), ("work", -3),
+    ("x", -5), ("x", 5), ("far", -6), ("work", 3), ("first", 6), ("first", -6), ("far", 6), ("x", -7), ("work", 4),
+    ("x", 7), ("x", 8), ("first", -5), ("first", 5), ("far", 5), ("far", -5), ("work", -6), ("work", 6), ("far", 7),
+    ("far", -7), ("first", -7), ("work", 5), ("work", -5), ("first", 7), ("far", 8), ("first", 8), ("work", -7),
+    ("work", 7), ("work", 8),
+)
+RING_ORDER = (
+    ("ring", 0, 0), ("ring", 0, 1), ("ring", 0, 2), ("ring", -1, 0), ("ring", 1, 0), ("ring", -1, 1), ("ring", 1, 1),
+    ("ring", 0, 3), ("ring", -1, 2), ("ring", 1, 2), ("ring", -3, 0), ("ring", 3, 0), ("ring", 3, 1), ("ring", -3, 1),
+    ("ring", 2, 0), ("ring", -2, 0), ("ring", -2, 1), ("ring", -3, 2), ("ring", 2, 1), ("ring", -1, 3),
+    ("ring", 3, 2), ("ring", 1, 3), ("ring", 4, 0), ("ring", -4, 0), ("ring", -3, 3), ("ring", 3, 3), ("ring", -4, 1),
+    ("ring", 4, 1), ("ring", 2, 2), ("ring", -2, 2), ("ring", -2, 3), ("ring", 2, 3), ("ring", 4, 2), ("ring", -4, 2),
+    ("ring", 5, 0), ("ring", 6, 0), ("ring", -5, 0), ("ring", 5, 1), ("ring", -4, 3), ("ring", 4, 3), ("ring", -5, 1),
+    ("ring", -6, 0), ("ring", 6, 1), ("ring", 5, 2), ("ring", -6, 1), ("ring", -5, 2), ("ring", 6, 2),
+    ("ring", -6, 2), ("ring", 7, 0), ("ring", -7, 0), ("ring", 8, 0), ("ring", 5, 3), ("ring", -5, 3),
+    ("ring", -6, 3), ("ring", -7, 1), ("ring", 7, 1), ("ring", 6, 3), ("ring", -7, 2), ("sum", 0, 0), ("ring", 8, 1),
+    ("ring", 7, 2), ("ring", 8, 2), ("sum", 0, 1), ("ring", -7, 3), ("ring", 7, 3), ("sum", 0, 2), ("ring", 8, 3),
+    ("sum", 0, 3),
+)
 
 
 def sends_of(plan, offset):
@@ -37,20 +63,6 @@
     return [k for pair in zip(up, down) for k in pair] if offset == 0 else up + down
 
 
-def gather_events():
-    pieces = [(0.0, 0)] + [(t, o) for o, t in BLOCK_TIME.items()] + [(t, -o) for o, t in BLOCK_TIME.items() if o < NZ // 2]
-    pieces.sort()
-    events = [(6.0, 5, 0, "slots"), (7.0, 5, 0, "spread")]
-    near = far = 0.0
-    for t, o in pieces:
-        near = max(near + 0.9, t + 2.8)
-        far = max(far + 1.0, near + 2.8)
-        if o:
-            events.append((t, 0, o, "z"))
-        events += [(near, 1, o, "x"), (far, 2, o, "far"), (far + 2.0, 3, o, "work")]
-    return [(kind, o) for _, _, o, kind in sorted(events)]
-
-
 def iota(shape, dim):
     return lax.broadcasted_iota(jnp.int32, shape, dim)
 
@@ -61,17 +73,6 @@
 
 def dot(a, b):
     return jnp.dot(a, b, preferred_element_type=F32)
-
-
-def ring_events():
-    events = []
-    for eb in range(N_EB):
-        events.append((1.5 * eb, eb, 0, "ring"))
-        for o, t in RING_TIME.items():
-            for signed in (o, -o) if o < NZ // 2 else (o,):
-                events.append((t + eb + 1.0, eb, signed, "ring"))
-        events.append((RING_TIME[NZ // 2] + eb + 3.0, eb, 0, "sum"))
-    return [(kind, o, eb) for _, eb, o, kind in sorted(events)]
 
 
 def kernel(
@@ -117,6 +118,8 @@
     s_recv,
     n_recv,
     z_recv,
+    f_recv,
+    fx_recv,
     xw_recv,
     xh_recv,
     core_recv,
@@ -155,7 +158,7 @@
 
     barrier = pltpu.get_barrier_semaphore()
     offsets = [(dx, dy) for dx in range(NX) for dy in range(NY) if dx or dy]
-    z_steps = sorted({k for plan in (BLOCK_PLAN, RING_PLAN) for steps in plan.values() for k in steps})
+    z_steps = sorted({k for plan in (BLOCK_PLAN, FIRST_PLAN, RING_PLAN) for steps in plan.values() for k in steps})
     greeted = [at_z(k) for step in z_steps for k in (step, -step)] + [mate] + [at_xy(dx, dy) for dx, dy in offsets]
     for device in greeted:
         pl.semaphore_signal(barrier, inc=1, device_id=device, device_id_type=MESH)
@@ -196,43 +199,56 @@
     def z_of_piece(o):
         return lax.rem(z - o + NZ, NZ)
 
+    rest, first_rows = pl.ds(FIRST, REST), pl.ds(0, FIRST)
+
     def z_piece(o):
         zz = z_of_piece(o)
-        piece = blocks.at[x, zz, c]
+        piece = blocks.at[x, zz, c, rest, :]
         if o:
             await_bytes(piece, z_recv.at[zz])
         for k in sends_of(BLOCK_PLAN, o):
             send_piece(piece, send_sem.at[0], z_recv.at[zz], at_z(k))
-        send_piece(piece, send_sem.at[1], xw_recv.at[0, zz], x_up)
-        send_piece(piece, send_sem.at[1], xw_recv.at[1, zz], x_down)
+        send_piece(piece, send_sem.at[1], xw_recv.at[zz], x_up)
+        send_piece(piece, send_sem.at[1], xw_recv.at[zz], x_down)
         send_piece(piece, send_sem.at[2], core_recv.at[zz], mate)
 
+    def first_piece(o):
+        zz = z_of_piece(o)
+        piece = blocks.at[:, zz, c, first_rows, :]
+        if o:
+            await_bytes(piece, f_recv.at[zz])
+        else:
+            await_bytes(blocks.at[pl.ds(0, NX - 1), z, c, first_rows, :], fx_recv)
+        for k in sends_of(FIRST_PLAN, o):
+            send_piece(piece, send_sem.at[11], f_recv.at[zz], at_z(k))
+        send_piece(piece, send_sem.at[2], core_recv.at[zz], mate)
+
     xl, xr, xo = lax.rem(x + NX - 1, NX), lax.rem(x + 1, NX), lax.rem(x + 2, NX)
+
+    def halves(o):
+        cut = FIRST + (2 * REST // 3 if o % 2 else REST // 3)
+        return pl.ds(FIRST, cut - FIRST), pl.ds(cut, SL - cut)
 
     def x_piece(o):
         zz = z_of_piece(o)
-        await_bytes(blocks.at[xl, zz, c], xw_recv.at[0, zz])
-        low = blocks.at[xl, zz, c, pl.ds(0, HALF), :]
-        send_piece(low, send_sem.at[1], xh_recv.at[0, zz], x_up)
-        send_piece(blocks.at[xl, zz, c], send_sem.at[2], core_recv.at[zz], mate)
-        await_bytes(blocks.at[xr, zz, c], xw_recv.at[1, zz])
-        high = blocks.at[xr, zz, c, pl.ds(HALF, HALF), :]
-        send_piece(high, send_sem.at[1], xh_recv.at[1, zz], x_down)
-        send_piece(blocks.at[xr, zz, c], send_sem.at[2], core_recv.at[zz], mate)
+        low, high = halves(o)
+        await_bytes(blocks.at[pl.ds(0, 2), zz, c, rest, :], xw_recv.at[zz])
+        send_piece(blocks.at[xl, zz, c, low, :], send_sem.at[1], xh_recv.at[zz], x_up)
+        send_piece(blocks.at[xr, zz, c, high, :], send_sem.at[1], xh_recv.at[zz], x_down)
+        send_piece(blocks.at[xl, zz, c, rest, :], send_sem.at[2], core_recv.at[zz], mate)
+        send_piece(blocks.at[xr, zz, c, rest, :], send_sem.at[2], core_recv.at[zz], mate)
 
     def far_piece(o):
         zz = z_of_piece(o)
-        await_bytes(blocks.at[xo, zz, c, pl.ds(0, HALF), :], xh_recv.at[0, zz])
-        await_bytes(blocks.at[xo, zz, c, pl.ds(HALF, HALF), :], xh_recv.at[1, zz])
-        send_piece(blocks.at[xo, zz, c], send_sem.at[2], core_recv.at[zz], mate)
+        piece = blocks.at[xo, zz, c, rest, :]
+        await_bytes(piece, xh_recv.at[zz])
+        send_piece(piece, send_sem.at[2], core_recv.at[zz], mate)
 
     group = BLK8 * CAP
 
     def slot_rows():
-        for dy in range(1, NY):
-            other = lax.rem(y + NY - dy, NY)
-            await_bytes(slot_all.at[other], s_recv.at[dy])
-            await_bytes(amp_all.at[other], y_recv.at[dy])
+        await_bytes(slot_all.at[pl.ds(0, NY - 1)], s_recv)
+        await_bytes(amp_all.at[pl.ds(0, NY - 1)], y_recv)
         for q in range(NY):
             slot_of = slot_all[q, 0:1, :]
             here = slot_of == iota((NZ * group, ROWS), 0).astype(F32)
@@ -244,8 +260,7 @@
                 slotted[:, pl.ds(q * group, group), pl.ds(p * V, V)] = part.reshape(NZ, group, V)
 
     def spread_counts():
-        for dx in range(1, NX):
-            await_bytes(counts.at[lax.rem(x + NX - dx, NX)], n_recv.at[dx])
+        await_bytes(counts.at[pl.ds(0, NX - 1)], n_recv)
         n_out = NX * 4
         tall = iota((n_out * EB, NX * 16), 0) // EB
         pick_row = (iota((n_out * EB, NX * 16), 1) == (tall // 4) * 16 + lax.rem(tall, 4)).astype(F32).astype(BF16)
@@ -273,21 +288,23 @@
             prod = jnp.where(lane_block == k, raw[k * SL : (k + 1) * SL], prod)
         inter_acc[...] += dot(prod.astype(BF16), rows)
 
+    for dx in range(1, NX):
+        send_piece(blocks.at[x, z, c, first_rows, :], send_sem.at[12], fx_recv, at_xy(dx, 0))
     z_piece(0)
     for dy in range(1, NY):
-        send_piece(slot_all.at[y], send_sem.at[3], s_recv.at[dy], at_xy(0, dy))
-        send_piece(amp_all.at[y], send_sem.at[4], y_recv.at[dy], at_xy(0, dy))
+        send_piece(slot_all.at[y], send_sem.at[3], s_recv, at_xy(0, dy))
+        send_piece(amp_all.at[y], send_sem.at[4], y_recv, at_xy(0, dy))
     for dx in range(1, NX):
-        send_piece(counts.at[x], send_sem.at[5], n_recv.at[dx], at_xy(dx, 0))
+        send_piece(counts.at[x], send_sem.at[5], n_recv, at_xy(dx, 0))
     inter_acc[...] = jnp.zeros_like(inter_acc)
 
-    for kind, o in gather_events():
+    for kind, o in GATHER_ORDER:
         if kind == "slots":
             slot_rows()
         elif kind == "spread":
             spread_counts()
         else:
-            {"z": z_piece, "x": x_piece, "far": far_piece, "work": block_work}[kind](o)
+            {"z": z_piece, "first": first_piece, "x": x_piece, "far": far_piece, "work": block_work}[kind](o)
 
     for eb in range(N_EB):
         for p in range(2):
@@ -326,11 +343,11 @@
                 w_send.at[there["pairs_0"], there["ints"], eb],
                 w_recv.at[dx, dy, eb],
                 send_sem.at[8 if dx else 10],
-                w_rsem.at[dx, dy],
+                w_rsem.at[1 if dx else 0],
                 there,
             ).start()
 
-    for kind, o, eb in ring_events():
+    for kind, o, eb in RING_ORDER:
         if kind == "ring":
             ring_piece(o, eb)
         else:
@@ -339,8 +356,8 @@
     w_recv[0, 0] = w_send[x, y]
     for i in (1, 8, 9):
         copies[i].wait()
-    for dx, dy in offsets:
-        await_bytes(w_recv.at[dx, dy], w_rsem.at[dx, dy])
+    await_bytes(w_recv.at[0, pl.ds(1, NY - 1)], w_rsem.at[0])
+    await_bytes(w_recv.at[pl.ds(1, NX - 1)], w_rsem.at[1])
 
     lane_low = iota((SL, 128), 1) < SL
     for p in range(2):
@@ -368,9 +385,8 @@
         m_send[q] = joined.astype(BF16)
     for dy in range(NY):
         there = at_xy(NX // 2, dy)
-        remote(m_send.at[there["ints"]], m_recv.at[dy], send_sem.at[9], m_rsem.at[dy], there).start()
-    for dy in range(NY):
-        await_bytes(m_recv.at[dy], m_rsem.at[dy])
+        remote(m_send.at[there["ints"]], m_recv.at[dy], send_sem.at[9], m_rsem, there).start()
+    await_bytes(m_recv, m_rsem)
     mirror = jnp.concatenate([m_recv[lax.rem(y - q + NY, NY)].astype(F32) for q in range(NY)], axis=0)
     mirror = jnp.transpose(mirror)
     first_twin = ((xo * NZ + z) * NC + c) * 2
@@ -379,8 +395,10 @@
         other = jnp.where(which == 1, mirror[SL:], mirror[:SL])
         out_ref[p] = -0.5 * (scaled[p] + other)
 
-    await_bytes(blocks.at[0, pl.ds(0, NZ - 1), 0], send_sem.at[0])
-    await_bytes(blocks.at[pl.ds(0, NX - 1), :, 0], send_sem.at[1])
+    await_bytes(blocks.at[0, pl.ds(0, NZ - 1), 0, rest, :], send_sem.at[0])
+    await_bytes(blocks.at[pl.ds(0, NX - 1), :, 0, rest, :], send_sem.at[1])
+    await_bytes(blocks.at[:, pl.ds(0, NZ - 1), 0, first_rows, :], send_sem.at[11])
+    await_bytes(blocks.at[pl.ds(0, NX - 1), 0, 0, first_rows, :], send_sem.at[12])
     await_bytes(blocks.at[:, :, 0], send_sem.at[2])
     await_bytes(slot_all.at[pl.ds(0, NY - 1)], send_sem.at[3])
     await_bytes(amp_all.at[pl.ds(0, NY - 1)], send_sem.at[4])
@@ -409,7 +427,7 @@
     return pl.pallas_call(
         kernel,
         out_shape=jax.ShapeDtypeStruct((2, SL, V), F32),
-        in_specs=[pl.BlockSpec(memory_space=pl.ANY)] * 10,
+        in_specs=[pl.BlockSpec(memory_space=pltpu.HBM)] * 10,
         out_specs=pl.BlockSpec(memory_space=pltpu.VMEM),
         scratch_shapes=[
             pltpu.VMEM((V, V), F32),
@@ -438,32 +456,39 @@
             pltpu.SMEM((2,), F32),
             pltpu.SMEM((2,), jnp.int32),
             dma((10,)),
-            dma((11,)),
-            dma((NY,)),
-            dma((NY,)),
-            dma((NX,)),
+            dma((13,)),
+            dma,
+            dma,
+            dma,
             dma((NZ,)),
-            dma((2, NZ)),
-            dma((2, NZ)),
+            dma((NZ,)),
+            dma,
+            dma((NZ,)),
+            dma((NZ,)),
             dma((NZ,)),
             dma((N_EB, NZ)),
             dma((N_EB,)),
-            dma((NX, NY)),
-            dma((NY,)),
+            dma((2,)),
+            dma,
         ],
-        compiler_params=pltpu.CompilerParams(collective_id=0, has_side_effects=True),
+        compiler_params=pltpu.CompilerParams(collective_id=0, has_side_effects=True, vmem_limit_bytes=24 * 2**20),
         name="cycle",
     )(
-        amps.reshape(ROWS, V),
-        resid_rest,
-        int_blocks[0],
-        virt_energy,
-        item_block.reshape(1, -1),
-        share_owner.reshape(1, -1),
-        share_pair.reshape(1, -1),
-        share_amp.reshape(1, -1),
-        pair_energy,
-        transpose_pair,
+        *(
+            pltpu.with_memory_space_constraint(operand, pltpu.HBM)
+            for operand in (
+                amps.reshape(ROWS, V),
+                resid_rest,
+                int_blocks[0],
+                virt_energy,
+                item_block.reshape(1, -1),
+                share_owner.reshape(1, -1),
+                share_pair.reshape(1, -1),
+                share_amp.reshape(1, -1),
+                pair_energy,
+                transpose_pair,
+            )
+        )
     )
 
 

time: 85.1 us -> 78.4 us (0.921)
  Pallas kernels: 83.4 us -> 77.6 us
  local copies, waits for them, and re-layouts: 1.57 us -> 0.66 us
    pallas_call x1, Pallas kernels: 83.4 us -> 77.6 us  [body(): pl.pallas_call(kernel, out_shape=jax.ShapeDtypeStruct((2, SL, V), F32), i...]
    unnamed x1, local copies, waits for them, and re-layouts: 1.57 us -> 0.66 us
where the time goes in v3:
time: 78.4 us; the launch traced here: 78.3 us
  Pallas kernels  77.6 us (99%)
    pallas_call x1, Pallas kernels, body(): pl.pallas_call(kernel, out_shape=jax.ShapeDtypeStruct((2, SL, V), F32), i...  77.6 us

profile of v3, /device:TPU:1, one launch (start us, length us, event | category | flops | bytes accessed | tf_op | source)
XLA Modules:
  0.0 78.3 jit_solution(2979698642909315847)
XLA Ops:
  0.0 77.6 %cycle.1 = f32[2,64,256]{2,1,0:T(8,128)S(1)} custom-call(f32[128,256]{1,0:T(8,128)} %bitcast.6, f32[2,64,256]{2,1,0:T(8,128)} %resid_hbm.1, bf16[256,256]{1,0:T(8,128)(2,1)} %bitcast.7, f32[2,256]{1,0:T(2,128)} %energy_hbm.1, s32[1,64]{1,0:T(1,128)} %bitcast.8, s32[1,96]{1,0:T(1,128)} %bitcast.9, s32[1,96]{1,0:T(1,128)} %bitcast.10, s32[1,96]{1,0:T(1,128)} %bitcast.11, ...), custom_call_target="tpu_custom_call" | custom-call | tf_op jit(solution)/shard_map/cycle/pallas_call | solution.py:427
  77.6 0.7 copy.12

commit v4 on v3

--- a/solution.py
+++ b/solution.py
@@ -30,28 +30,28 @@
 FIRST_PLAN = {0: (1,), 1: (3, 1), 2: (1,), 3: (2,), 4: (2,), 6: (2, 1)}
 RING_PLAN = {0: (3, 1), 1: (1,), 3: (1,), 4: (2, 1), 6: (2, 1)}
 GATHER_ORDER = (
-    ("z", -1), ("z", 1), ("x", 0), ("first", 0), ("z", 3), ("z", -3), ("slots", 0), ("z", 2), ("z", -2),
-    ("spread", 0), ("x", 1), ("first", -1), ("first", 1), ("x", -1), ("far", 0), ("z", -4), ("z", 4), ("x", 3),
-    ("work", 0), ("x", -3), ("x", 2), ("x", -2), ("z", -6), ("z", 6), ("far", 1), ("far", -1), ("first", 2),
-    ("first", -2), ("x", -4), ("x", 4), ("work", 1), ("far", 3), ("far", -3), ("work", -1), ("z", -5), ("far", 2),
-    ("z", 5), ("first", 4), ("x", -6), ("first", -4), ("x", 6), ("z", -7), ("z", 7), ("far", -2), ("far", -4),
-    ("work", 2), ("first", -3), ("first", 3), ("far", 4), ("work", -2), ("z", 8), ("work", -4), ("work", -3),
-    ("x", -5), ("x", 5), ("far", -6), ("work", 3), ("first", 6), ("first", -6), ("far", 6), ("x", -7), ("work", 4),
-    ("x", 7), ("x", 8), ("first", -5), ("first", 5), ("far", 5), ("far", -5), ("work", -6), ("work", 6), ("far", 7),
-    ("far", -7), ("first", -7), ("work", 5), ("work", -5), ("first", 7), ("far", 8), ("first", 8), ("work", -7),
-    ("work", 7), ("work", 8),
+    ("z", -1), ("z", 1), ("first", 0), ("x", 0), ("z", 3), ("z", -3), ("spread", 0), ("z", 2), ("z", -2), ("x", 1),
+    ("first", 1), ("x", -1), ("first", -1), ("far", 0), ("slots", 0), ("z", 4), ("z", -4), ("x", 2), ("x", 3),
+    ("x", -2), ("x", -3), ("work", 0), ("z", -6), ("z", 6), ("far", 1), ("far", -1), ("first", -2), ("x", -4),
+    ("first", 2), ("x", 4), ("work", 1), ("z", 5), ("z", -5), ("far", 2), ("first", 4), ("far", -3), ("first", -4),
+    ("x", -6), ("z", -7), ("work", -1), ("far", 3), ("z", 7), ("x", 6), ("far", -4), ("far", -2), ("work", 2),
+    ("far", 4), ("first", -3), ("z", 8), ("first", 3), ("x", 5), ("x", -5), ("work", -3), ("far", -6), ("first", 6),
+    ("work", -4), ("x", -7), ("work", -2), ("x", 7), ("first", -6), ("work", 3), ("x", 8), ("work", 4), ("first", -5),
+    ("far", 6), ("first", 5), ("far", 5), ("far", -5), ("work", 6), ("work", -6), ("far", -7), ("far", 7),
+    ("first", -7), ("first", 7), ("work", 5), ("far", 8), ("first", 8), ("work", -5), ("work", -7), ("work", 7),
+    ("work", 8),
 )
 RING_ORDER = (
-    ("ring", 0, 0), ("ring", 0, 1), ("ring", 0, 2), ("ring", -1, 0), ("ring", 1, 0), ("ring", -1, 1), ("ring", 1, 1),
-    ("ring", 0, 3), ("ring", -1, 2), ("ring", 1, 2), ("ring", -3, 0), ("ring", 3, 0), ("ring", 3, 1), ("ring", -3, 1),
-    ("ring", 2, 0), ("ring", -2, 0), ("ring", -2, 1), ("ring", -3, 2), ("ring", 2, 1), ("ring", -1, 3),
-    ("ring", 3, 2), ("ring", 1, 3), ("ring", 4, 0), ("ring", -4, 0), ("ring", -3, 3), ("ring", 3, 3), ("ring", -4, 1),
-    ("ring", 4, 1), ("ring", 2, 2), ("ring", -2, 2), ("ring", -2, 3), ("ring", 2, 3), ("ring", 4, 2), ("ring", -4, 2),
-    ("ring", 5, 0), ("ring", 6, 0), ("ring", -5, 0), ("ring", 5, 1), ("ring", -4, 3), ("ring", 4, 3), ("ring", -5, 1),
-    ("ring", -6, 0), ("ring", 6, 1), ("ring", 5, 2), ("ring", -6, 1), ("ring", -5, 2), ("ring", 6, 2),
-    ("ring", -6, 2), ("ring", 7, 0), ("ring", -7, 0), ("ring", 8, 0), ("ring", 5, 3), ("ring", -5, 3),
-    ("ring", -6, 3), ("ring", -7, 1), ("ring", 7, 1), ("ring", 6, 3), ("ring", -7, 2), ("sum", 0, 0), ("ring", 8, 1),
-    ("ring", 7, 2), ("ring", 8, 2), ("sum", 0, 1), ("ring", -7, 3), ("ring", 7, 3), ("sum", 0, 2), ("ring", 8, 3),
+    ("ring", 0, 0), ("ring", 0, 1), ("ring", 0, 2), ("ring", -1, 1), ("ring", -1, 0), ("ring", 1, 0), ("ring", 1, 1),
+    ("ring", 0, 3), ("ring", -1, 2), ("ring", -3, 0), ("ring", 3, 0), ("ring", 1, 2), ("ring", 3, 1), ("ring", -3, 1),
+    ("ring", -3, 2), ("ring", -2, 0), ("ring", 2, 0), ("ring", 3, 2), ("ring", -2, 1), ("ring", -1, 3),
+    ("ring", 1, 3), ("ring", 2, 1), ("ring", 4, 0), ("ring", -4, 0), ("ring", 3, 3), ("ring", -3, 3), ("ring", -2, 2),
+    ("ring", 2, 2), ("ring", -4, 1), ("ring", 4, 1), ("ring", 2, 3), ("ring", 4, 2), ("ring", -4, 2), ("ring", 6, 0),
+    ("ring", -4, 3), ("ring", -5, 0), ("ring", 4, 3), ("ring", -2, 3), ("ring", -6, 0), ("ring", 5, 0),
+    ("ring", -5, 1), ("ring", 5, 1), ("ring", 6, 1), ("ring", 5, 2), ("ring", -6, 1), ("ring", 6, 2), ("ring", -6, 2),
+    ("ring", 7, 0), ("ring", -5, 2), ("ring", -7, 0), ("ring", 8, 0), ("ring", -5, 3), ("ring", -6, 3),
+    ("ring", 6, 3), ("ring", -7, 1), ("ring", 7, 1), ("sum", 0, 0), ("ring", 5, 3), ("ring", 8, 1), ("ring", 7, 2),
+    ("ring", -7, 2), ("ring", 8, 2), ("sum", 0, 1), ("ring", -7, 3), ("sum", 0, 2), ("ring", 7, 3), ("ring", 8, 3),
     ("sum", 0, 3),
 )
 
@@ -150,18 +150,19 @@
     def await_bytes(ref, sem):
         pltpu.make_async_copy(ref, ref, sem).wait()
 
+    barrier = pltpu.get_barrier_semaphore()
+    offsets = [(dx, dy) for dx in range(NX) for dy in range(NY) if dx or dy]
+    z_steps = sorted({k for plan in (BLOCK_PLAN, FIRST_PLAN, RING_PLAN) for steps in plan.values() for k in steps})
+    greeted = [at_xy(dx, dy) for dx, dy in sorted(offsets, key=lambda d: d[0] % 2 + d[1] % 2)]
+    greeted += [at_z(k) for step in z_steps[::-1] for k in (step, -step)] + [mate]
+    for device in greeted:
+        pl.semaphore_signal(barrier, inc=1, device_id=device, device_id_type=MESH)
+
     held = (amps_hbm, resid_hbm, block_hbm, energy_hbm, item_hbm, owner_hbm, pair_hbm, mate_hbm, pair_energy_hbm, twin_hbm)
     used = (amps_ref, resid, block_ref, energy_ref, item_ref, owner_ref, pair_ref, mate_ref, pair_energy_ref, twin_ref)
     copies = [pltpu.make_async_copy(a, b, local_sem.at[i]) for i, (a, b) in enumerate(zip(held, used))]
     for i in (2, 0, 4, 5, 6, 7, 3, 8, 9, 1):
         copies[i].start()
-
-    barrier = pltpu.get_barrier_semaphore()
-    offsets = [(dx, dy) for dx in range(NX) for dy in range(NY) if dx or dy]
-    z_steps = sorted({k for plan in (BLOCK_PLAN, FIRST_PLAN, RING_PLAN) for steps in plan.values() for k in steps})
-    greeted = [at_z(k) for step in z_steps for k in (step, -step)] + [mate] + [at_xy(dx, dy) for dx, dy in offsets]
-    for device in greeted:
-        pl.semaphore_signal(barrier, inc=1, device_id=device, device_id_type=MESH)
 
     copies[2].wait()
     turned[...] = jnp.transpose(block_ref[...].astype(F32))

time: 78.4 us -> 77.6 us (0.990)
  Pallas kernels: 77.6 us -> 76.8 us
    pallas_call x1, Pallas kernels: 77.6 us -> 76.8 us  [body(): pl.pallas_call(kernel, out_shape=jax.ShapeDtypeStruct((2, SL, V), F32), i...]
where the time goes in v4:
time: 77.6 us; the launch traced here: 77.4 us
  Pallas kernels  76.8 us (99%)
    pallas_call x1, Pallas kernels, body(): pl.pallas_call(kernel, out_shape=jax.ShapeDtypeStruct((2, SL, V), F32), i...  76.8 us

profile of v4, /device:TPU:1, one launch (start us, length us, event | category | flops | bytes accessed | tf_op | source)
XLA Modules:
  0.0 77.4 jit_solution(16669218377352015789)
XLA Ops:
  0.0 76.8 %cycle.1 = f32[2,64,256]{2,1,0:T(8,128)S(1)} custom-call(f32[128,256]{1,0:T(8,128)} %bitcast.6, f32[2,64,256]{2,1,0:T(8,128)} %resid_hbm.1, bf16[256,256]{1,0:T(8,128)(2,1)} %bitcast.7, f32[2,256]{1,0:T(2,128)} %energy_hbm.1, s32[1,64]{1,0:T(1,128)} %bitcast.8, s32[1,96]{1,0:T(1,128)} %bitcast.9, s32[1,96]{1,0:T(1,128)} %bitcast.10, s32[1,96]{1,0:T(1,128)} %bitcast.11, ...), custom_call_target="tpu_custom_call" | custom-call | tf_op jit(solution)/shard_map/cycle/pallas_call | solution.py:428
  76.8 0.7 copy.12

commit v5 on v4

--- a/solution.py
+++ b/solution.py
@@ -30,29 +30,28 @@
 FIRST_PLAN = {0: (1,), 1: (3, 1), 2: (1,), 3: (2,), 4: (2,), 6: (2, 1)}
 RING_PLAN = {0: (3, 1), 1: (1,), 3: (1,), 4: (2, 1), 6: (2, 1)}
 GATHER_ORDER = (
-    ("z", -1), ("z", 1), ("first", 0), ("x", 0), ("z", 3), ("z", -3), ("spread", 0), ("z", 2), ("z", -2), ("x", 1),
-    ("first", 1), ("x", -1), ("first", -1), ("far", 0), ("slots", 0), ("z", 4), ("z", -4), ("x", 2), ("x", 3),
-    ("x", -2), ("x", -3), ("work", 0), ("z", -6), ("z", 6), ("far", 1), ("far", -1), ("first", -2), ("x", -4),
-    ("first", 2), ("x", 4), ("work", 1), ("z", 5), ("z", -5), ("far", 2), ("first", 4), ("far", -3), ("first", -4),
-    ("x", -6), ("z", -7), ("work", -1), ("far", 3), ("z", 7), ("x", 6), ("far", -4), ("far", -2), ("work", 2),
-    ("far", 4), ("first", -3), ("z", 8), ("first", 3), ("x", 5), ("x", -5), ("work", -3), ("far", -6), ("first", 6),
-    ("work", -4), ("x", -7), ("work", -2), ("x", 7), ("first", -6), ("work", 3), ("x", 8), ("work", 4), ("first", -5),
-    ("far", 6), ("first", 5), ("far", 5), ("far", -5), ("work", 6), ("work", -6), ("far", -7), ("far", 7),
-    ("first", -7), ("first", 7), ("work", 5), ("far", 8), ("first", 8), ("work", -5), ("work", -7), ("work", 7),
+    ("x", 0), ("z", -1), ("z", 1), ("first", 0), ("z", 3), ("z", -3), ("spread", 0), ("z", 2), ("z", -2),
+    ("first", 1), ("x", 1), ("x", -1), ("first", -1), ("z", -4), ("z", 4), ("x", -3), ("x", 3), ("x", 2), ("z", -6),
+    ("x", -2), ("far", 0), ("slots", 0), ("z", 6), ("far", 1), ("far", -1), ("x", -4), ("first", 2), ("first", -2),
+    ("x", 4), ("z", 5), ("work", -1), ("z", -5), ("far", -3), ("far", 2), ("first", 4), ("x", -6), ("work", 0),
+    ("z", -7), ("x", 6), ("first", -4), ("far", -4), ("z", 7), ("far", 3), ("far", -2), ("work", 1), ("work", 2),
+    ("far", 4), ("first", 3), ("z", 8), ("first", -3), ("x", 5), ("work", -4), ("work", -2), ("x", -5), ("far", -6),
+    ("first", 6), ("x", -7), ("work", 3), ("x", 7), ("first", -6), ("work", 4), ("far", 6), ("x", 8), ("work", -3),
+    ("first", 5), ("far", 5), ("first", -5), ("far", -5), ("work", -6), ("work", 6), ("work", 5), ("far", 7),
+    ("far", -7), ("first", 7), ("first", -7), ("first", 8), ("far", 8), ("work", -5), ("work", 7), ("work", -7),
     ("work", 8),
 )
 RING_ORDER = (
-    ("ring", 0, 0), ("ring", 0, 1), ("ring", 0, 2), ("ring", -1, 1), ("ring", -1, 0), ("ring", 1, 0), ("ring", 1, 1),
-    ("ring", 0, 3), ("ring", -1, 2), ("ring", -3, 0), ("ring", 3, 0), ("ring", 1, 2), ("ring", 3, 1), ("ring", -3, 1),
-    ("ring", -3, 2), ("ring", -2, 0), ("ring", 2, 0), ("ring", 3, 2), ("ring", -2, 1), ("ring", -1, 3),
-    ("ring", 1, 3), ("ring", 2, 1), ("ring", 4, 0), ("ring", -4, 0), ("ring", 3, 3), ("ring", -3, 3), ("ring", -2, 2),
-    ("ring", 2, 2), ("ring", -4, 1), ("ring", 4, 1), ("ring", 2, 3), ("ring", 4, 2), ("ring", -4, 2), ("ring", 6, 0),
-    ("ring", -4, 3), ("ring", -5, 0), ("ring", 4, 3), ("ring", -2, 3), ("ring", -6, 0), ("ring", 5, 0),
-    ("ring", -5, 1), ("ring", 5, 1), ("ring", 6, 1), ("ring", 5, 2), ("ring", -6, 1), ("ring", 6, 2), ("ring", -6, 2),
-    ("ring", 7, 0), ("ring", -5, 2), ("ring", -7, 0), ("ring", 8, 0), ("ring", -5, 3), ("ring", -6, 3),
-    ("ring", 6, 3), ("ring", -7, 1), ("ring", 7, 1), ("sum", 0, 0), ("ring", 5, 3), ("ring", 8, 1), ("ring", 7, 2),
-    ("ring", -7, 2), ("ring", 8, 2), ("sum", 0, 1), ("ring", -7, 3), ("sum", 0, 2), ("ring", 7, 3), ("ring", 8, 3),
-    ("sum", 0, 3),
+    ("ring", 0, 0), ("ring", 0, 1), ("ring", 0, 2), ("ring", -1, 0), ("ring", 1, 0), ("ring", -1, 1), ("ring", 1, 1),
+    ("ring", 0, 3), ("ring", 3, 0), ("ring", -3, 0), ("ring", 1, 2), ("ring", 3, 1), ("ring", -3, 1), ("ring", 2, 0),
+    ("ring", -1, 2), ("ring", -2, 0), ("ring", -2, 1), ("ring", -3, 2), ("ring", -1, 3), ("ring", 3, 2),
+    ("ring", 1, 3), ("ring", 4, 0), ("ring", -4, 0), ("ring", -3, 3), ("ring", 3, 3), ("ring", 2, 1), ("ring", 2, 2),
+    ("ring", -4, 1), ("ring", 4, 1), ("ring", -2, 2), ("ring", 4, 2), ("ring", 2, 3), ("ring", -4, 2), ("ring", 6, 0),
+    ("ring", -5, 0), ("ring", -6, 0), ("ring", -4, 3), ("ring", 5, 1), ("ring", 4, 3), ("ring", -2, 3),
+    ("ring", 6, 1), ("ring", -6, 1), ("ring", 5, 0), ("ring", -6, 2), ("ring", 5, 2), ("ring", -5, 1), ("ring", 6, 2),
+    ("ring", 7, 0), ("ring", -7, 0), ("ring", 8, 0), ("ring", 5, 3), ("ring", -6, 3), ("ring", 6, 3), ("ring", -5, 2),
+    ("ring", -7, 1), ("ring", -5, 3), ("ring", 7, 1), ("ring", -7, 2), ("ring", 8, 1), ("sum", 0, 0), ("ring", 8, 2),
+    ("ring", 7, 2), ("sum", 0, 1), ("ring", -7, 3), ("sum", 0, 2), ("ring", 7, 3), ("ring", 8, 3), ("sum", 0, 3),
 )
 
 
@@ -167,31 +166,6 @@
     copies[2].wait()
     turned[...] = jnp.transpose(block_ref[...].astype(F32))
     blocks[x, z, c] = turned[pl.ds(pl.multiple_of(y * SL, SL), SL), :].astype(BF16)
-    copies[0].wait()
-    amp_all[y] = amps_ref[...].astype(BF16)
-
-    copies[4].wait()
-    n_items = item_ref.shape[1]
-    twice = (iota((n_items, ROWS), 0) == iota((n_items, ROWS), 1) // 2).astype(F32).astype(BF16)
-    item = jnp.broadcast_to(item_ref[...].astype(F32), (16, n_items)).astype(BF16)
-    row = dot(item, twice)[0:1].astype(jnp.int32)
-    square = jnp.broadcast_to(row, (ROWS, ROWS)).astype(F32)
-    earlier = (jnp.transpose(square) == square) & (iota((ROWS, ROWS), 0) < iota((ROWS, ROWS), 1))
-    rank = jnp.sum(earlier.astype(F32), axis=0, keepdims=True)
-    z_of = (row >> 1) & (NZ - 1)
-    place = z_of * (BLK8 * CAP) + ((row >> 5) * NC + (row & 1)) * CAP
-    slot_all[y] = jnp.broadcast_to(place.astype(F32) + rank, (8, ROWS))
-
-    for i in (5, 6, 7):
-        copies[i].wait()
-    n_req = owner_ref.shape[1]
-    unit = owner_ref[...] * 2 + pair_ref[...]
-    hot = (iota((V, n_req), 0) == unit).astype(F32).astype(BF16)
-    out_id = iota((16, n_req), 0)
-    mine = (iota((16, n_req), 1) // (n_req // 2)) * 2 + mate_ref[...]
-    pick = (out_id == mine).astype(F32).astype(BF16)
-    counts[x] = dot_nt(pick, hot).astype(BF16)
-
     pl.semaphore_wait(barrier, len(greeted))
 
     def send_piece(ref, ssem, rsem, device):
@@ -266,11 +240,14 @@
         tall = iota((n_out * EB, NX * 16), 0) // EB
         pick_row = (iota((n_out * EB, NX * 16), 1) == (tall // 4) * 16 + lax.rem(tall, 4)).astype(F32).astype(BF16)
         tall_counts = dot(pick_row, counts[...].reshape(NX * 16, V)).astype(BF16)
-        wide = iota((V, UNITS * EB), 1) // EB + x * UNITS
-        pick_col = (iota((V, UNITS * EB), 0) == wide).astype(F32).astype(BF16)
-        full = dot(tall_counts, pick_col)
-        same = lax.rem(iota(full.shape, 0), EB) == lax.rem(iota(full.shape, 1), EB)
-        spread[...] = jnp.where(same, full, 0.0).astype(BF16)
+        half = UNITS // NC * EB
+        place = iota((V, half), 1) // EB
+        for core in range(NC):
+            wide = (place // 2) * (NC * 2) + core * 2 + lax.rem(place, 2) + x * UNITS
+            pick_col = (iota((V, half), 0) == wide).astype(F32).astype(BF16)
+            full = dot(tall_counts, pick_col)
+            same = lax.rem(iota(full.shape, 0), EB) == lax.rem(iota(full.shape, 1), EB)
+            spread[core] = jnp.where(same, full, 0.0).astype(BF16)
         copies[3].wait()
         for p in range(2):
             ecol[p] = jnp.transpose(jnp.broadcast_to(energy_ref[p : p + 1, :], (128, V)))
@@ -292,6 +269,31 @@
     for dx in range(1, NX):
         send_piece(blocks.at[x, z, c, first_rows, :], send_sem.at[12], fx_recv, at_xy(dx, 0))
     z_piece(0)
+    copies[0].wait()
+    amp_all[y] = amps_ref[...].astype(BF16)
+
+    copies[4].wait()
+    n_items = item_ref.shape[1]
+    twice = (iota((n_items, ROWS), 0) == iota((n_items, ROWS), 1) // 2).astype(F32).astype(BF16)
+    item = jnp.broadcast_to(item_ref[...].astype(F32), (16, n_items)).astype(BF16)
+    row = dot(item, twice)[0:1].astype(jnp.int32)
+    square = jnp.broadcast_to(row, (ROWS, ROWS)).astype(F32)
+    earlier = (jnp.transpose(square) == square) & (iota((ROWS, ROWS), 0) < iota((ROWS, ROWS), 1))
+    rank = jnp.sum(earlier.astype(F32), axis=0, keepdims=True)
+    z_of = (row >> 1) & (NZ - 1)
+    place = z_of * (BLK8 * CAP) + ((row >> 5) * NC + (row & 1)) * CAP
+    slot_all[y] = jnp.broadcast_to(place.astype(F32) + rank, (8, ROWS))
+
+    for i in (5, 6, 7):
+        copies[i].wait()
+    n_req = owner_ref.shape[1]
+    unit = owner_ref[...] * 2 + pair_ref[...]
+    hot = (iota((V, n_req), 0) == unit).astype(F32).astype(BF16)
+    out_id = iota((16, n_req), 0)
+    mine = (iota((16, n_req), 1) // (n_req // 2)) * 2 + mate_ref[...]
+    pick = (out_id == mine).astype(F32).astype(BF16)
+    counts[x] = dot_nt(pick, hot).astype(BF16)
+
     for dy in range(1, NY):
         send_piece(slot_all.at[y], send_sem.at[3], s_recv, at_xy(0, dy))
         send_piece(amp_all.at[y], send_sem.at[4], y_recv, at_xy(0, dy))
@@ -323,9 +325,10 @@
     low_lane = iota((EB, 128), 1) < SL
 
     def sum_part(eb):
+        half = UNITS // NC * EB
+        sums = dot(spread[c], inter[eb, :, c].reshape(half, V))
         await_bytes(inter.at[eb, :, 1 - c], gc_recv.at[eb])
-        part = inter[eb].reshape(UNITS * EB, V)
-        sums = dot(spread[...], part)
+        sums += dot(spread[1 - c], inter[eb, :, 1 - c].reshape(half, V))
         for xd in range(NX):
             for p in range(2):
                 base = (xd * 4 + p * 2) * EB
@@ -436,7 +439,7 @@
             pltpu.VMEM((NY, ROWS, V), BF16),
             pltpu.VMEM((NY, 8, ROWS), F32),
             pltpu.VMEM((NX, 16, V), BF16),
-            pltpu.VMEM((NX * 4 * EB, UNITS * EB), BF16),
+            pltpu.VMEM((NC, NX * 4 * EB, UNITS // NC * EB), BF16),
             pltpu.VMEM((NZ, SLOTS, 2 * V), BF16),
             pltpu.VMEM((SL, 2 * V), F32),
             pltpu.VMEM((N_EB, NZ, NC, 2, EB, V), BF16),

time: 77.6 us -> 77.7 us (level)
  no operation moved by 1% of the time
where the time goes in v5:
time: 77.7 us; the launch traced here: 77.5 us
  Pallas kernels  76.9 us (99%)
    pallas_call x1, Pallas kernels, body(): pl.pallas_call(kernel, out_shape=jax.ShapeDtypeStruct((2, SL, V), F32), i...  76.9 us

profile of v5, /device:TPU:1, one launch (start us, length us, event | category | flops | bytes accessed | tf_op | source)
XLA Modules:
  0.0 77.5 jit_solution(9323400923077717417)
XLA Ops:
  0.0 76.9 %cycle.1 = f32[2,64,256]{2,1,0:T(8,128)S(1)} custom-call(f32[128,256]{1,0:T(8,128)} %bitcast.6, f32[2,64,256]{2,1,0:T(8,128)} %resid_hbm.1, bf16[256,256]{1,0:T(8,128)(2,1)} %bitcast.7, f32[2,256]{1,0:T(2,128)} %energy_hbm.1, s32[1,64]{1,0:T(1,128)} %bitcast.8, s32[1,96]{1,0:T(1,128)} %bitcast.9, s32[1,96]{1,0:T(1,128)} %bitcast.10, s32[1,96]{1,0:T(1,128)} %bitcast.11, ...), custom_call_target="tpu_custom_call" | custom-call | tf_op jit(solution)/shard_map/cycle/pallas_call | solution.py:431
  76.9 0.7 copy.12
